TPU v7x, 32 devices: a whole 2x2x4 slice. The times are simulated.
32 devices in a mesh: bricks: 8 (over z, y), group: 4 (over x, core).
Axes of the slice: x: 2, y: 2, z: 4, core: 2. Of those that a mesh axis runs over, the one named last changes fastest.
Arguments:
- right_side: float32 [3, 128, 64, 128], P(None, 'bricks', 'group'), may hold values from -6 to 6
- material: int32 [128, 64, 128], P('bricks', 'group'), may hold values from 0 to 3
- brick_level: int32 [8, 4], P('bricks', 'group'), may hold values from 0 to 2
- mortar_rows: int32 [8, 4, 16], P('bricks', 'group'), may hold values from 0 to 15, each once within a row
- material_mu: float32 [4], replicated, may hold values from 0.5 to 4
- material_lam: float32 [4], replicated, may hold values from 0.25 to 2
- coarse_inverse: float32 [8, 48, 48], P('bricks'), may hold values from -1 to 5, as said below
Outputs:
- solution: float32 [3, 128, 64, 128], P(None, 'bricks', 'group')
- residual: float32 [3, 128, 64, 128], P(None, 'bricks', 'group')
Inputs may be any that keep to these rules, and one draw needn't show every extreme that they name: `coarse_inverse`: each brick row's matrix is of full rank with a positive diagonal.
All inputs are finite; a program needn't handle non-finite values.
Results may differ from a plain program's by a relative error of at most 0.00027.
Values sent between devices are 32-bit elements; how exact they have to be, the bound alone decides.
A program may use at most 64 MiB of HBM per device.

v0:
```python
import jax
import jax.numpy as jnp
from jax import lax
from jax.sharding import PartitionSpec as P

BLOCK_XY = 16
BLOCK_Z = 32
CHEB = 4


low_ratio = 0.15
bound_margin = 1.1


def shifted(block, axis, distance):
    devices = range(lax.axis_size(axis))
    route = [(i - distance, i) for i in devices if i - distance in devices]
    return lax.ppermute(block, axis, route)


def padded_2(block, sides, width):
    for axis, dim in sides:
        count = lax.axis_size(axis)
        forward = [(i, i + 1) for i in range(count - 1)]
        backward = [(target, source) for source, target in forward]
        low = lax.ppermute(
            lax.slice_in_dim(block, block.shape[dim] - width, None, axis=dim), axis, forward
        )
        high = lax.ppermute(lax.slice_in_dim(block, 0, width, axis=dim), axis, backward)
        block = jnp.concatenate([low, block, high], axis=dim)
    return block


def lookup(ids, table):
    total = jnp.zeros(ids.shape, table.dtype)
    for entry in range(4):
        total = total + jnp.where(ids == entry, table[entry], 0.0)
    return total


def chebyshev(solution, residual, apply, diagonal, lower, upper):
    theta = 0.5 * (upper + lower)
    delta = 0.5 * (upper - lower)
    sigma = theta / delta
    damping = 1.0 / sigma
    update = residual / (diagonal * theta)
    for turn in range(CHEB):
        solution = solution + update
        residual = residual - apply(update)
        if turn + 1 < CHEB:
            damping_next = 1.0 / (2.0 * sigma - damping)
            update = damping_next * damping * update + 2.0 * damping_next / delta * (
                residual / diagonal
            )
            damping = damping_next
    return (solution, residual)


def per_device(
    right_side, material, brick_level, mortar_rows, material_mu, material_lam, coarse_inverse
):
    brick_count = lax.axis_size("bricks")
    group_count = lax.axis_size("group")
    brick_index = lax.axis_index("bricks")
    group_index = lax.axis_index("group")
    depth_x, width_y, width_z = material.shape
    order = mortar_rows[0, 0]

    def neighbours(field, sides):
        last_face = field[:, -1]
        first_face = field[:, 0]
        below = shifted(last_face[:, order], "bricks", 1)
        received = shifted(first_face, "bricks", -1)
        above = jnp.zeros_like(received).at[:, order].set(received)
        sides = padded_2(field, (("group", 2),), 1)
        x_plus = jnp.concatenate([field[:, 1:], above[:, None]], axis=1)
        x_minus = jnp.concatenate([below[:, None], field[:, :-1]], axis=1)
        y_plus = sides[:, :, 2:]
        y_minus = sides[:, :, :-2]
        z_plus = jnp.pad(field[:, :, :, 1:], ((0, 0), (0, 0), (0, 0), (0, 1)))
        z_minus = jnp.pad(field[:, :, :, :-1], ((0, 0), (0, 0), (0, 0), (1, 0)))
        return [x_plus, x_minus, y_plus, y_minus, z_plus, z_minus]

    level_scale = jnp.exp2(2.0 * brick_level[0, 0].astype(right_side.dtype))
    shear = lookup(material, material_mu) * level_scale
    bulk = lookup(material, material_lam) * level_scale
    x_index = lax.broadcasted_iota(jnp.int32, material.shape, 0)
    y_index = lax.broadcasted_iota(jnp.int32, material.shape, 1)
    z_index = lax.broadcasted_iota(jnp.int32, material.shape, 2)
    outside = [
        (brick_index == brick_count - 1) & (x_index == depth_x - 1),
        (brick_index == 0) & (x_index == 0),
        (group_index == group_count - 1) & (y_index == width_y - 1),
        (group_index == 0) & (y_index == 0),
        z_index == width_z - 1,
        z_index == 0,
    ]
    shear_near = neighbours(shear[None], None)
    weights = [
        jnp.where(edge, shear, 0.5 * (shear + other[0])) for edge, other in zip(outside, shear_near)
    ]
    weight_total = weights[0]
    for extra in weights[1:]:
        weight_total = weight_total + extra
    diagonal = weight_total + 1.5 * bulk
    bound_ratio = (2.0 * weight_total + 2.5 * bulk) / diagonal
    upper = bound_margin * lax.pmax(jnp.max(bound_ratio), ("bricks", "group"))
    lower = low_ratio * upper

    def apply(field, sides=None):
        near = neighbours(field, sides)
        coupled = jnp.sum(field, axis=0)
        result = weight_total * field + bulk * (field + 0.5 * coupled)
        for weight, value in zip(weights, near):
            result = result - weight * value
        return result

    solution = jnp.zeros_like(right_side)
    solution, residual = chebyshev(solution, right_side, apply, diagonal, lower, upper)
    cells_x = depth_x // BLOCK_XY
    cells_y = width_y // BLOCK_XY
    cells_z = width_z // BLOCK_Z
    own_coarse = jnp.mean(
        residual.reshape(3, cells_x, BLOCK_XY, cells_y, BLOCK_XY, cells_z, BLOCK_Z), axis=(2, 4, 6)
    ).reshape(-1)
    piece_size = own_coarse.shape[0]
    inverse_rows = coarse_inverse[0]
    offset = group_index * piece_size
    whole = None
    padded = lax.dynamic_update_slice_in_dim(
        jnp.zeros((inverse_rows.shape[0],), own_coarse.dtype), own_coarse, offset, 0
    )
    whole = lax.psum(padded, "group")
    correction = jnp.dot(
        lax.dynamic_slice_in_dim(inverse_rows, offset, piece_size, 0),
        whole,
        precision=lax.Precision.HIGHEST,
    )
    blocky = correction.reshape(3, cells_x, cells_y, cells_z)
    fine = jnp.broadcast_to(
        blocky[:, :, None, :, None, :, None],
        (3, cells_x, BLOCK_XY, cells_y, BLOCK_XY, cells_z, BLOCK_Z),
    ).reshape(right_side.shape)
    fine_layers = None
    solution = solution + fine
    residual = residual - apply(fine, fine_layers)
    solution, residual = chebyshev(solution, residual, apply, diagonal, lower, upper)
    return (solution, residual)


def solution(mesh):
    return jax.shard_map(
        per_device,
        mesh=mesh,
        in_specs=(
            P(None, "bricks", "group", None),
            P("bricks", "group", None),
            P("bricks", "group"),
            P("bricks", "group", None),
            P(),
            P(),
            P("bricks", None, None),
        ),
        out_specs=(P(None, "bricks", "group", None), P(None, "bricks", "group", None)),
        check_vma=False,
    )
```

profile of v0, /device:TPU:0, one launch (start us, length us, event | category | flops | bytes accessed | tf_op | source)
XLA Modules:
  0.0 269.2 jit_solution(2325039186035003641)
XLA Ops:
  2.8 3.5 %fusion.106 = (f32[1,16,16,128]{3,2,1,0:T(8,128)S(1)}, pred[16,16,128]{2,1,0:T(8,128)(4,1)S(1)}, pred[16,16,128]{2,1,0:T(8,128)(4,1)S(1)}, pred[16,16,128]{2,1,0:T(8,128)(4,1)S(1)}, pred[16,16,128]{2,1,0:T(8,128)(4,1)S(1)}) fusion(f32[]{:T(128)} %bitcast.4, f32[]{:T(128)} %bitcast.3, f32[]{:T(128)} %bitcast.2, f32[]{:T(128)} %bitcast.1, f32[]{:T(128)} %bitcast, ...), kind=kLoop, calls=%fused_computation.227 | loop fusion | flops 393216 | bytes 393236 | tf_op jit(solution)/shard_map/broadcast_in_dim | solution.py:98
  7.5 4.9 %collective-permute-start.1 = (f32[1,16,128]{2,1,0:T(8,128)S(1)}, f32[1,16,128]{2,1,0:T(8,128)S(1)}, u32[]{:S(2)}, u32[]{:S(2)}) collective-permute-start(f32[1,16,128]{2,1,0:T(8,128)S(1)} %bitcast.188), channel_id=1, source_target_pairs={{0,4},{4,8},{8,12},{12,16},{16,20},{20,24},{24,28},{1,5},{5,9},{9,... | collective-permute-start | bytes 24584 | tf_op jit(solution)/shard_map/ppermute | solution.py:18
  23.0 3.3 %fusion.98 = (f32[]{:T(128)}, f32[16,16,128]{2,1,0:T(8,128)S(1)}, f32[16,16,128]{2,1,0:T(8,128)S(1)}) fusion(f32[16,16,128]{2,1,0:T(8,128)S(1)} %get-tuple-element.36, f32[16,16,128]{2,1,0:T(8,128)S(1)} %get-tuple-element.31, f32[16,16,128]{2,1,0:T(8,128)S(1)} %get-tuple-element.30, f32[]{:T(128)} %bitcast.4, ...), kind=kLoop, calls=%fused_computation.176 | loop fusion | flops 557055 | bytes 786456 | tf_op jit(solution)/shard_map/reduce_max | solution.py:107
  26.2 42.2 %pmax.7 = f32[]{:T(128)} all-reduce(f32[]{:T(128)} %get-tuple-element.39), channel_id=1, replica_groups=mesh['bricks'=8,'group'=4] {'bricks','group'}, use_global_device_ids=true, to_apply=%region_2.3 | all-reduce | flops 1 | bytes 8 | tf_op jit(solution)/shard_map/pmax | solution.py:107
  74.7 5.0 %collective-permute-start.5 = (f32[3,16,128]{2,0,1:T(4,128)S(1)}, f32[3,16,128]{2,0,1:T(4,128)S(1)}, u32[]{:S(2)}, u32[]{:S(2)}) collective-permute-start(f32[3,16,128]{2,0,1:T(4,128)S(1)} %bitcast.171), channel_id=1, source_target_pairs={{0,4},{4,8},{8,12},{12,16},{16,20},{20,24},{24,28},{1,5},{5,9},{9,... | collective-permute-start | bytes 73736 | tf_op jit(solution)/shard_map/ppermute | solution.py:18
  86.1 3.8 %fusion.121 = (f32[16,16,128]{2,1,0:T(8,128)}, f32[3,16,16,128]{3,0,2,1:T(4,128)S(1)}, f32[3,16,16,128]{3,0,2,1:T(4,128)S(1)}) fusion(f32[16,16,128]{2,1,0:T(8,128)S(1)} %get-tuple-element.40, f32[]{:T(128)S(6)} %div.48, f32[3,16,16,128]{3,0,2,1:T(4,128)S(1)} %get-tuple-element.38, f32[]{:T(128)S(6)} %mul.326, f32[3,16,16,127]{3,0,2,1:T(4,128)} %get-tuple-element.110, ...), kind=kLoop, calls=%fused_computation.235 | loop fusion | flops 2523136 | bytes 4630536 | tf_op jit(solution)/shard_map/reduce_sum | solution.py:112
  94.6 5.4 %collective-permute-start.9 = (f32[3,16,128]{2,0,1:T(4,128)S(1)}, f32[3,16,128]{2,0,1:T(4,128)S(1)}, u32[]{:S(2)}, u32[]{:S(2)}) collective-permute-start(f32[3,16,128]{2,0,1:T(4,128)S(1)} %bitcast.174), channel_id=1, source_target_pairs={{0,4},{4,8},{8,12},{12,16},{16,20},{20,24},{24,28},{1,5},{5,9},{9,... | collective-permute-start | bytes 73736 | tf_op jit(solution)/shard_map/ppermute | solution.py:18
  114.2 5.3 %collective-permute-start.13 = (f32[3,16,128]{2,0,1:T(4,128)S(1)}, f32[3,16,128]{2,0,1:T(4,128)S(1)}, u32[]{:S(2)}, u32[]{:S(2)}) collective-permute-start(f32[3,16,128]{2,0,1:T(4,128)S(1)} %bitcast.175), channel_id=1, source_target_pairs={{0,4},{4,8},{8,12},{12,16},{16,20},{20,24},{24,28},{1,5},{5,9},{9,... | collective-permute-start | bytes 73736 | tf_op jit(solution)/shard_map/ppermute | solution.py:18
  120.8 4.6 %collective-permute-start.15 = (f32[3,16,1,128]{3,0,2,1:T(4,128)S(1)}, f32[3,16,1,128]{3,0,2,1:T(4,128)S(1)}, u32[]{:S(2)}, u32[]{:S(2)}) collective-permute-start(f32[3,16,1,128]{3,0,2,1:T(4,128)S(1)} %get-tuple-element.92), channel_id=1, source_target_pairs={{0,1},{1,2},{2,3},{4,5},{5,6},{6,7},{8,9},{9,10},{10,11},{12,13},{... | collective-permute-start | bytes 73736 | tf_op jit(solution)/shard_map/ppermute | solution.py:26
  127.7 3.5 %fusion.117 = (f32[16,16,128]{2,1,0:T(8,128)S(1)}, f32[3,16,16,128]{3,0,2,1:T(4,128)S(1)}, f32[3,16,16,128]{3,0,2,1:T(4,128)}) fusion(f32[16,16,128]{2,1,0:T(8,128)S(1)} %get-tuple-element.40, f32[]{:T(128)S(6)} %div.105, f32[3,16,16,128]{3,0,2,1:T(4,128)S(1)} %get-tuple-element.24, f32[]{:T(128)S(6)} %mul.364, ...), kind=kLoop, calls=%fused_computation.233 | loop fusion | flops 2523136 | bytes 4630536 | tf_op jit(solution)/shard_map/reduce_sum | solution.py:112
  137.6 5.2 %collective-permute-start.17 = (f32[3,16,128]{2,0,1:T(4,128)}, f32[3,16,128]{2,0,1:T(4,128)S(1)}, u32[]{:S(2)}, u32[]{:S(2)}) collective-permute-start(f32[3,16,128]{2,0,1:T(4,128)} %bitcast.46), channel_id=1, source_target_pairs={{0,4},{4,8},{8,12},{12,16},{16,20},{20,24},{24,28},{1,5},{5,9},{9,... | collective-permute-start | bytes 73736 | tf_op jit(solution)/shard_map/ppermute | solution.py:18
  144.0 4.4 %collective-permute-start.19 = (f32[3,16,1,128]{3,0,2,1:T(4,128)}, f32[3,16,1,128]{3,0,2,1:T(4,128)S(1)}, u32[]{:S(2)}, u32[]{:S(2)}) collective-permute-start(f32[3,16,1,128]{3,0,2,1:T(4,128)} %get-tuple-element.84), channel_id=1, source_target_pairs={{0,1},{1,2},{2,3},{4,5},{5,6},{6,7},{8,9},{9,10},{10,11},{12,13},{... | collective-permute-start | bytes 73736 | tf_op jit(solution)/shard_map/ppermute | solution.py:26
  153.8 7.5 %psum.7 = f32[48]{0:T(128)S(1)} all-reduce(f32[48]{0:T(128)S(1)} %dynamic_update_slice.3), channel_id=1, replica_groups=mesh['bricks'=8,'group'=4] {'group'}, use_global_device_ids=true, to_apply=%region_13.14 | all-reduce | flops 48 | bytes 384 | tf_op jit(solution)/shard_map/psum | solution.py:133
  168.2 5.4 %collective-permute-start.21 = (f32[3,16,128]{2,0,1:T(4,128)S(1)}, f32[3,16,128]{2,0,1:T(4,128)S(1)}, u32[]{:S(2)}, u32[]{:S(2)}) collective-permute-start(f32[3,16,128]{2,0,1:T(4,128)S(1)} %bitcast.172), channel_id=1, source_target_pairs={{0,4},{4,8},{8,12},{12,16},{16,20},{20,24},{24,28},{1,5},{5,9},{9,... | collective-permute-start | bytes 73736 | tf_op jit(solution)/shard_map/ppermute | solution.py:18
  183.7 5.4 %collective-permute-start.25 = (f32[3,16,128]{2,0,1:T(4,128)S(1)}, f32[3,16,128]{2,0,1:T(4,128)S(1)}, u32[]{:S(2)}, u32[]{:S(2)}) collective-permute-start(f32[3,16,128]{2,0,1:T(4,128)S(1)} %bitcast.176), channel_id=1, source_target_pairs={{0,4},{4,8},{8,12},{12,16},{16,20},{20,24},{24,28},{1,5},{5,9},{9,... | collective-permute-start | bytes 73736 | tf_op jit(solution)/shard_map/ppermute | solution.py:18
  195.9 4.2 %fusion.111 = (f32[16,16,128]{2,1,0:T(8,128)}, f32[3,16,16,128]{3,0,2,1:T(4,128)S(1)}, f32[3,16,16,128]{3,0,2,1:T(4,128)}) fusion(f32[16,16,128]{2,1,0:T(8,128)} %copy-done.17, f32[]{:T(128)S(6)} %div.48, f32[3,16,16,128]{3,0,2,1:T(4,128)S(1)} %get-tuple-element.16, f32[]{:T(128)S(6)} %mul.326, f32[3,16,16,128]{3,0,2,1:T(4,128)} %get-tuple-element.17, ...), kind=kLoop, calls=%fused_computation.230 | loop fusion | flops 2523136 | bytes 4630536 | tf_op jit(solution)/shard_map/reduce_sum | solution.py:112
  204.7 5.7 %collective-permute-start.29 = (f32[3,16,128]{2,0,1:T(4,128)S(1)}, f32[3,16,128]{2,0,1:T(4,128)S(1)}, u32[]{:S(2)}, u32[]{:S(2)}) collective-permute-start(f32[3,16,128]{2,0,1:T(4,128)S(1)} %bitcast.177), channel_id=1, source_target_pairs={{0,4},{4,8},{8,12},{12,16},{16,20},{20,24},{24,28},{1,5},{5,9},{9,... | collective-permute-start | bytes 73736 | tf_op jit(solution)/shard_map/ppermute | solution.py:18
  211.7 3.7 %collective-permute-start.31 = (f32[3,16,1,128]{3,0,2,1:T(4,128)S(1)}, f32[3,16,1,128]{3,0,2,1:T(4,128)S(1)}, u32[]{:S(2)}, u32[]{:S(2)}) collective-permute-start(f32[3,16,1,128]{3,0,2,1:T(4,128)S(1)} %get-tuple-element.68), channel_id=1, source_target_pairs={{0,1},{1,2},{2,3},{4,5},{5,6},{6,7},{8,9},{9,10},{10,11},{12,13},{... | collective-permute-start | bytes 73736 | tf_op jit(solution)/shard_map/ppermute | solution.py:26
  217.8 4.3 %fusion.109 = (f32[16,16,128]{2,1,0:T(8,128)}, f32[3,16,16,128]{3,0,2,1:T(4,128)S(1)}, f32[3,16,16,128]{3,0,2,1:T(4,128)}) fusion(f32[16,16,128]{2,1,0:T(8,128)} %copy-done.17, f32[]{:T(128)S(6)} %div.102, f32[3,16,16,128]{3,0,2,1:T(4,128)S(1)} %get-tuple-element.13, f32[]{:T(128)S(6)} %mul.349, f32[3,16,16,128]{3,0,2,1:T(4,128)} %get-tuple-element.14, ...), kind=kLoop, calls=%fused_computation.229 | loop fusion | flops 2523136 | bytes 4630536 | tf_op jit(solution)/shard_map/reduce_sum | solution.py:112
  226.6 5.2 %collective-permute-start.33 = (f32[3,16,128]{2,0,1:T(4,128)S(1)}, f32[3,16,128]{2,0,1:T(4,128)S(1)}, u32[]{:S(2)}, u32[]{:S(2)}) collective-permute-start(f32[3,16,128]{2,0,1:T(4,128)S(1)} %bitcast.178), channel_id=1, source_target_pairs={{0,4},{4,8},{8,12},{12,16},{16,20},{20,24},{24,28},{1,5},{5,9},{9,... | collective-permute-start | bytes 73736 | tf_op jit(solution)/shard_map/ppermute | solution.py:18
  233.1 4.4 %collective-permute-start.35 = (f32[3,16,1,128]{3,0,2,1:T(4,128)S(1)}, f32[3,16,1,128]{3,0,2,1:T(4,128)S(1)}, u32[]{:S(2)}, u32[]{:S(2)}) collective-permute-start(f32[3,16,1,128]{3,0,2,1:T(4,128)S(1)} %get-tuple-element.60), channel_id=1, source_target_pairs={{0,1},{1,2},{2,3},{4,5},{5,6},{6,7},{8,9},{9,10},{10,11},{12,13},{... | collective-permute-start | bytes 73736 | tf_op jit(solution)/shard_map/ppermute | solution.py:26
  239.8 4.3 %fusion.107 = (f32[16,16,128]{2,1,0:T(8,128)}, f32[3,16,16,128]{3,0,2,1:T(4,128)S(1)}, f32[3,16,16,128]{3,0,2,1:T(4,128)}) fusion(f32[16,16,128]{2,1,0:T(8,128)} %copy-done.17, f32[]{:T(128)S(6)} %div.105, f32[3,16,16,128]{3,0,2,1:T(4,128)S(1)} %get-tuple-element.10, f32[]{:T(128)S(6)} %mul.364, f32[3,16,16,128]{3,0,2,1:T(4,128)} %get-tuple-element.11, ...), kind=kLoop, calls=%fused_computation.228 | loop fusion | flops 2523136 | bytes 4630536 | tf_op jit(solution)/shard_map/reduce_sum | solution.py:112
  250.8 5.2 %collective-permute-start.37 = (f32[3,16,128]{2,0,1:T(4,128)S(1)}, f32[3,16,128]{2,0,1:T(4,128)S(1)}, u32[]{:S(2)}, u32[]{:S(2)}) collective-permute-start(f32[3,16,128]{2,0,1:T(4,128)S(1)} %bitcast.173), channel_id=1, source_target_pairs={{0,4},{4,8},{8,12},{12,16},{16,20},{20,24},{24,28},{1,5},{5,9},{9,... | collective-permute-start | bytes 73736 | tf_op jit(solution)/shard_map/ppermute | solution.py:18
  257.3 4.4 %collective-permute-start.39 = (f32[3,16,1,128]{3,0,2,1:T(4,128)S(1)}, f32[3,16,1,128]{3,0,2,1:T(4,128)S(1)}, u32[]{:S(2)}, u32[]{:S(2)}) collective-permute-start(f32[3,16,1,128]{3,0,2,1:T(4,128)S(1)} %get-tuple-element.54), channel_id=1, source_target_pairs={{0,1},{1,2},{2,3},{4,5},{5,6},{6,7},{8,9},{9,10},{10,11},{12,13},{... | collective-permute-start | bytes 73736 | tf_op jit(solution)/shard_map/ppermute | solution.py:26
  (252 shorter events, 114.1 us)
Async XLA Ops:
  7.5 12.7 %collective-permute-start.1 = (f32[1,16,128]{2,1,0:T(8,128)S(1)}, f32[1,16,128]{2,1,0:T(8,128)S(1)}, u32[]{:S(2)}, u32[]{:S(2)}) collective-permute-start(f32[1,16,128]{2,1,0:T(8,128)S(1)} %bitcast.188), channel_id=1, source_target_pairs={{0,4},{4,8},{8,12},{12,16},{16,20},{20,24},{24,28},{1,5},{5,9},{9,... | collective-permute-start | bytes 24584 | tf_op jit(solution)/shard_map/ppermute | solution.py:18
  72.8 11.6 %collective-permute-start.4 = (f32[3,16,128]{2,0,1:T(4,128)S(1)}, f32[3,16,128]{2,0,1:T(4,128)S(1)}, u32[]{:S(2)}, u32[]{:S(2)}) collective-permute-start(f32[3,16,128]{2,0,1:T(4,128)S(1)} %get-tuple-element.105), channel_id=1, source_target_pairs={{4,0},{8,4},{12,8},{16,12},{20,16},{24,20},{28,24},{5,1},{9,5},{13... | collective-permute-start | bytes 73736 | tf_op jit(solution)/shard_map/ppermute | solution.py:18
  74.7 10.8 %collective-permute-start.5 = (f32[3,16,128]{2,0,1:T(4,128)S(1)}, f32[3,16,128]{2,0,1:T(4,128)S(1)}, u32[]{:S(2)}, u32[]{:S(2)}) collective-permute-start(f32[3,16,128]{2,0,1:T(4,128)S(1)} %bitcast.171), channel_id=1, source_target_pairs={{0,4},{4,8},{8,12},{12,16},{16,20},{20,24},{24,28},{1,5},{5,9},{9,... | collective-permute-start | bytes 73736 | tf_op jit(solution)/shard_map/ppermute | solution.py:18
  92.5 12.7 %collective-permute-start.8 = (f32[3,16,128]{2,0,1:T(4,128)S(1)}, f32[3,16,128]{2,0,1:T(4,128)S(1)}, u32[]{:S(2)}, u32[]{:S(2)}) collective-permute-start(f32[3,16,128]{2,0,1:T(4,128)S(1)} %get-tuple-element.97), channel_id=1, source_target_pairs={{4,0},{8,4},{12,8},{16,12},{20,16},{24,20},{28,24},{5,1},{9,5},{13... | collective-permute-start | bytes 73736 | tf_op jit(solution)/shard_map/ppermute | solution.py:18
  94.6 11.7 %collective-permute-start.9 = (f32[3,16,128]{2,0,1:T(4,128)S(1)}, f32[3,16,128]{2,0,1:T(4,128)S(1)}, u32[]{:S(2)}, u32[]{:S(2)}) collective-permute-start(f32[3,16,128]{2,0,1:T(4,128)S(1)} %bitcast.174), channel_id=1, source_target_pairs={{0,4},{4,8},{8,12},{12,16},{16,20},{20,24},{24,28},{1,5},{5,9},{9,... | collective-permute-start | bytes 73736 | tf_op jit(solution)/shard_map/ppermute | solution.py:18
  112.4 13.7 %collective-permute-start.12 = (f32[3,16,128]{2,0,1:T(4,128)S(1)}, f32[3,16,128]{2,0,1:T(4,128)S(1)}, u32[]{:S(2)}, u32[]{:S(2)}) collective-permute-start(f32[3,16,128]{2,0,1:T(4,128)S(1)} %get-tuple-element.89), channel_id=1, source_target_pairs={{4,0},{8,4},{12,8},{16,12},{20,16},{24,20},{28,24},{5,1},{9,5},{13... | collective-permute-start | bytes 73736 | tf_op jit(solution)/shard_map/ppermute | solution.py:18
  114.2 12.9 %collective-permute-start.13 = (f32[3,16,128]{2,0,1:T(4,128)S(1)}, f32[3,16,128]{2,0,1:T(4,128)S(1)}, u32[]{:S(2)}, u32[]{:S(2)}) collective-permute-start(f32[3,16,128]{2,0,1:T(4,128)S(1)} %bitcast.175), channel_id=1, source_target_pairs={{0,4},{4,8},{8,12},{12,16},{16,20},{20,24},{24,28},{1,5},{5,9},{9,... | collective-permute-start | bytes 73736 | tf_op jit(solution)/shard_map/ppermute | solution.py:18
  119.5 7.6 %collective-permute-start.14 = (f32[3,16,1,128]{3,0,2,1:T(4,128)S(1)}, f32[3,16,1,128]{3,0,2,1:T(4,128)S(1)}, u32[]{:S(2)}, u32[]{:S(2)}) collective-permute-start(f32[3,16,1,128]{3,0,2,1:T(4,128)S(1)} %get-tuple-element.91), channel_id=1, source_target_pairs={{1,0},{2,1},{3,2},{5,4},{6,5},{7,6},{9,8},{10,9},{11,10},{13,12},{... | collective-permute-start | bytes 73736 | tf_op jit(solution)/shard_map/ppermute | solution.py:29
  135.1 13.4 %collective-permute-start.16 = (f32[3,16,128]{2,0,1:T(4,128)}, f32[3,16,128]{2,0,1:T(4,128)}, u32[]{:S(2)}, u32[]{:S(2)}) collective-permute-start(f32[3,16,128]{2,0,1:T(4,128)} %get-tuple-element.81), channel_id=1, source_target_pairs={{4,0},{8,4},{12,8},{16,12},{20,16},{24,20},{28,24},{5,1},{9,5},{13... | collective-permute-start | bytes 73736 | tf_op jit(solution)/shard_map/ppermute | solution.py:18
  137.6 12.5 %collective-permute-start.17 = (f32[3,16,128]{2,0,1:T(4,128)}, f32[3,16,128]{2,0,1:T(4,128)S(1)}, u32[]{:S(2)}, u32[]{:S(2)}) collective-permute-start(f32[3,16,128]{2,0,1:T(4,128)} %bitcast.46), channel_id=1, source_target_pairs={{0,4},{4,8},{8,12},{12,16},{16,20},{20,24},{24,28},{1,5},{5,9},{9,... | collective-permute-start | bytes 73736 | tf_op jit(solution)/shard_map/ppermute | solution.py:18
  161.8 12.1 %collective-permute-start.20 = (f32[3,16,128]{2,0,1:T(4,128)S(1)}, f32[3,16,128]{2,0,1:T(4,128)S(1)}, u32[]{:S(2)}, u32[]{:S(2)}) collective-permute-start(f32[3,16,128]{2,0,1:T(4,128)S(1)} %squeeze.130), channel_id=1, source_target_pairs={{4,0},{8,4},{12,8},{16,12},{20,16},{24,20},{28,24},{5,1},{9,5},{13... | collective-permute-start | bytes 73736 | tf_op jit(solution)/shard_map/ppermute | solution.py:18
  163.7 11.6 %collective-permute-start.22 = (f32[3,16,1,128]{3,0,2,1:T(4,128)S(1)}, f32[3,16,1,128]{3,0,2,1:T(4,128)S(1)}, u32[]{:S(2)}, u32[]{:S(2)}) collective-permute-start(f32[3,16,1,128]{3,0,2,1:T(4,128)S(1)} %slice.397), channel_id=1, source_target_pairs={{1,0},{2,1},{3,2},{5,4},{6,5},{7,6},{9,8},{10,9},{11,10},{13,12},{... | collective-permute-start | bytes 73736 | tf_op jit(solution)/shard_map/ppermute | solution.py:29
  165.0 10.3 %collective-permute-start.23 = (f32[3,16,1,128]{3,0,2,1:T(4,128)S(1)}, f32[3,16,1,128]{3,0,2,1:T(4,128)S(1)}, u32[]{:S(2)}, u32[]{:S(2)}) collective-permute-start(f32[3,16,1,128]{3,0,2,1:T(4,128)S(1)} %slice.397), channel_id=1, source_target_pairs={{0,1},{1,2},{2,3},{4,5},{5,6},{6,7},{8,9},{9,10},{10,11},{12,13},{... | collective-permute-start | bytes 73736 | tf_op jit(solution)/shard_map/ppermute | solution.py:26
  181.8 12.4 %collective-permute-start.24 = (f32[3,16,128]{2,0,1:T(4,128)S(1)}, f32[3,16,128]{2,0,1:T(4,128)S(1)}, u32[]{:S(2)}, u32[]{:S(2)}) collective-permute-start(f32[3,16,128]{2,0,1:T(4,128)S(1)} %get-tuple-element.73), channel_id=1, source_target_pairs={{4,0},{8,4},{12,8},{16,12},{20,16},{24,20},{28,24},{5,1},{9,5},{13... | collective-permute-start | bytes 73736 | tf_op jit(solution)/shard_map/ppermute | solution.py:18
  183.7 11.6 %collective-permute-start.25 = (f32[3,16,128]{2,0,1:T(4,128)S(1)}, f32[3,16,128]{2,0,1:T(4,128)S(1)}, u32[]{:S(2)}, u32[]{:S(2)}) collective-permute-start(f32[3,16,128]{2,0,1:T(4,128)S(1)} %bitcast.176), channel_id=1, source_target_pairs={{0,4},{4,8},{8,12},{12,16},{16,20},{20,24},{24,28},{1,5},{5,9},{9,... | collective-permute-start | bytes 73736 | tf_op jit(solution)/shard_map/ppermute | solution.py:18
  202.7 13.4 %collective-permute-start.28 = (f32[3,16,128]{2,0,1:T(4,128)S(1)}, f32[3,16,128]{2,0,1:T(4,128)S(1)}, u32[]{:S(2)}, u32[]{:S(2)}) collective-permute-start(f32[3,16,128]{2,0,1:T(4,128)S(1)} %get-tuple-element.65), channel_id=1, source_target_pairs={{4,0},{8,4},{12,8},{16,12},{20,16},{24,20},{28,24},{5,1},{9,5},{13... | collective-permute-start | bytes 73736 | tf_op jit(solution)/shard_map/ppermute | solution.py:18
  204.7 12.5 %collective-permute-start.29 = (f32[3,16,128]{2,0,1:T(4,128)S(1)}, f32[3,16,128]{2,0,1:T(4,128)S(1)}, u32[]{:S(2)}, u32[]{:S(2)}) collective-permute-start(f32[3,16,128]{2,0,1:T(4,128)S(1)} %bitcast.177), channel_id=1, source_target_pairs={{0,4},{4,8},{8,12},{12,16},{16,20},{20,24},{24,28},{1,5},{5,9},{9,... | collective-permute-start | bytes 73736 | tf_op jit(solution)/shard_map/ppermute | solution.py:18
  224.6 13.6 %collective-permute-start.32 = (f32[3,16,128]{2,0,1:T(4,128)S(1)}, f32[3,16,128]{2,0,1:T(4,128)S(1)}, u32[]{:S(2)}, u32[]{:S(2)}) collective-permute-start(f32[3,16,128]{2,0,1:T(4,128)S(1)} %get-tuple-element.57), channel_id=1, source_target_pairs={{4,0},{8,4},{12,8},{16,12},{20,16},{24,20},{28,24},{5,1},{9,5},{13... | collective-permute-start | bytes 73736 | tf_op jit(solution)/shard_map/ppermute | solution.py:18
  226.6 12.6 %collective-permute-start.33 = (f32[3,16,128]{2,0,1:T(4,128)S(1)}, f32[3,16,128]{2,0,1:T(4,128)S(1)}, u32[]{:S(2)}, u32[]{:S(2)}) collective-permute-start(f32[3,16,128]{2,0,1:T(4,128)S(1)} %bitcast.178), channel_id=1, source_target_pairs={{0,4},{4,8},{8,12},{12,16},{16,20},{20,24},{24,28},{1,5},{5,9},{9,... | collective-permute-start | bytes 73736 | tf_op jit(solution)/shard_map/ppermute | solution.py:18
  231.8 7.4 %collective-permute-start.34 = (f32[3,16,1,128]{3,0,2,1:T(4,128)S(1)}, f32[3,16,1,128]{3,0,2,1:T(4,128)S(1)}, u32[]{:S(2)}, u32[]{:S(2)}) collective-permute-start(f32[3,16,1,128]{3,0,2,1:T(4,128)S(1)} %get-tuple-element.59), channel_id=1, source_target_pairs={{1,0},{2,1},{3,2},{5,4},{6,5},{7,6},{9,8},{10,9},{11,10},{13,12},{... | collective-permute-start | bytes 73736 | tf_op jit(solution)/shard_map/ppermute | solution.py:29
  248.9 15.7 %collective-permute-start.36 = (f32[3,16,128]{2,0,1:T(4,128)}, f32[3,16,128]{2,0,1:T(4,128)S(1)}, u32[]{:S(2)}, u32[]{:S(2)}) collective-permute-start(f32[3,16,128]{2,0,1:T(4,128)} %get-tuple-element.50), channel_id=1, source_target_pairs={{4,0},{8,4},{12,8},{16,12},{20,16},{24,20},{28,24},{5,1},{9,5},{13... | collective-permute-start | bytes 73736 | tf_op jit(solution)/shard_map/ppermute | solution.py:18
  250.8 14.8 %collective-permute-start.37 = (f32[3,16,128]{2,0,1:T(4,128)S(1)}, f32[3,16,128]{2,0,1:T(4,128)S(1)}, u32[]{:S(2)}, u32[]{:S(2)}) collective-permute-start(f32[3,16,128]{2,0,1:T(4,128)S(1)} %bitcast.173), channel_id=1, source_target_pairs={{0,4},{4,8},{8,12},{12,16},{16,20},{20,24},{24,28},{1,5},{5,9},{9,... | collective-permute-start | bytes 73736 | tf_op jit(solution)/shard_map/ppermute | solution.py:18
  256.0 9.7 %collective-permute-start.38 = (f32[3,16,1,128]{3,0,2,1:T(4,128)S(1)}, f32[3,16,1,128]{3,0,2,1:T(4,128)S(1)}, u32[]{:S(2)}, u32[]{:S(2)}) collective-permute-start(f32[3,16,1,128]{3,0,2,1:T(4,128)S(1)} %get-tuple-element.53), channel_id=1, source_target_pairs={{1,0},{2,1},{3,2},{5,4},{6,5},{7,6},{9,8},{10,9},{11,10},{13,12},{... | collective-permute-start | bytes 73736 | tf_op jit(solution)/shard_map/ppermute | solution.py:29
  257.3 8.4 %collective-permute-start.39 = (f32[3,16,1,128]{3,0,2,1:T(4,128)S(1)}, f32[3,16,1,128]{3,0,2,1:T(4,128)S(1)}, u32[]{:S(2)}, u32[]{:S(2)}) collective-permute-start(f32[3,16,1,128]{3,0,2,1:T(4,128)S(1)} %get-tuple-element.54), channel_id=1, source_target_pairs={{0,1},{1,2},{2,3},{4,5},{5,6},{6,7},{8,9},{9,10},{10,11},{12,13},{... | collective-permute-start | bytes 73736 | tf_op jit(solution)/shard_map/ppermute | solution.py:26
  (53 other events, 1467.4 us)
where the time goes:
time: 273 us; the launch traced here: 269 us
  starting transfers between devices  116 us (42%)
  local copies, waits for them, and re-layouts  51.2 us (19%)
  blocking collectives  49.7 us (18%)
  other arithmetic  47.3 us (17%)
  between operations  4.28 us (2%)
    ppermute x20, starting transfers between devices, shifted(): return lax.ppermute(block, axis, route)  65.9 us
    pmax x1, blocking collectives, per_device(): upper = bound_margin * lax.pmax(jnp.max(bound_ratio), ('bricks', 'group'))  42.2 us
    ppermute x10, starting transfers between devices, padded_2(): lax.ppermute(lax.slice_in_dim(block, block.shape[dim] - width, None, axis...  37.2 us
    reduce_sum x9, other arithmetic, apply(): coupled = jnp.sum(field, axis=0)  25.9 us
    ppermute x10, starting transfers between devices, padded_2(): lax.ppermute(lax.slice_in_dim(block, 0, width, axis=dim), axis, backward)  12.9 us
    slice x9, local copies, waits for them, and re-layouts, neighbours(): z_plus = jnp.pad(field[:, :, :, 1:], ((0, 0), (0, 0), (0, 0), (0, 1)))  10.5 us
    scatter x10, local copies, waits for them, and re-layouts, neighbours(): above = jnp.zeros_like(received).at[:, order].set(received)  10.3 us
    unnamed x76, local copies, waits for them, and re-layouts  9.03 us
  transfers between devices with their start and end apart: 40, of which 1 were waited for; matrix products, arithmetic and copies ran while one was open for 9% of the time, Pallas kernels for 0%

commit v1 on v0

v1 whole, which is shorter than its diff:
```python
import functools

import jax
import jax.numpy as jnp
from jax import lax
from jax.experimental import pallas as pl
from jax.experimental.pallas import tpu as pltpu
from jax.sharding import PartitionSpec as P

BLOCK_Z = 32
CHEB = 4
LOW_RATIO = 0.15
BOUND_MARGIN = 1.1
ROUNDS = 2 * CHEB
UNROLL = 4
HIGHEST = lax.Precision.HIGHEST


def kernel(
    nb, ng, dx, dy, dz,
    rhs, material, level, mortar, mu, lam, inverse,
    sol, res,
    u, r, shear, wx, wyp, wym, wzp, wzm, dg, hb, invd, coef, undo,
    s_send_up, s_send_y, s_recv, above, up_send, y_send, recv,
    m_own, m_all, m2_own, m2_all, c_own, c_all, f_all, fx_own, fx_recv,
    s_ssem, s_rsem, h_ssem, h_rsem,
    m_ssem, m_rsem, m2_ssem, m2_rsem, c_ssem, c_rsem, f_ssem, f_rsem,
):
    b = lax.axis_index("bricks")
    g = lax.axis_index("group")
    has = [b > 0, b < nb - 1, g > 0, g < ng - 1]
    sends = [has[1], has[0], has[3], has[2]]
    peers = [(b + 1, g), (b - 1, g), (b, g + 1), (b, g - 1)]

    def remote(src, dst, ssem, rsem, peer):
        return pltpu.make_async_remote_copy(
            src_ref=src, dst_ref=dst, send_sem=ssem, recv_sem=rsem,
            device_id=peer, device_id_type=pl.DeviceIdType.MESH,
        )

    barrier = pltpu.get_barrier_semaphore()
    others = [(b, lax.rem(g + k, ng)) for k in range(1, ng)]
    others += [(lax.rem(b + k, nb), g) for k in range(1, nb)]
    for peer in others:
        pl.semaphore_signal(
            barrier, inc=1, device_id=peer, device_id_type=pl.DeviceIdType.MESH
        )

    scale = jnp.where(level[0, 0] == 0, 1.0, jnp.where(level[0, 0] == 1, 4.0, 16.0))
    zero_face = jnp.zeros((3, dx, dz), jnp.float32)

    order = [mortar[0, 0, k] for k in range(dy)]
    for k in range(dy):
        total = jnp.int32(0)
        for j in range(dy):
            total = jnp.where(order[j] == k, jnp.int32(j), total)
        undo[k] = total

    def lookup(ids, table):
        total = jnp.where(ids == 0, table[0] * scale, 0.0)
        for entry in range(1, 4):
            total = jnp.where(ids == entry, table[entry] * scale, total)
        return total

    def shear_plane(i, _):
        ids = material[i]
        plane = lookup(ids, mu)
        shear[i + 1] = plane
        hb[i] = lookup(ids, lam)
        s_send_y[0, pl.ds(i, 1), :] = plane[dy - 1 : dy]
        s_send_y[1, pl.ds(i, 1), :] = plane[0:1]
        return 0

    lax.fori_loop(0, dx, shear_plane, 0, unroll=UNROLL)
    for k in range(dy):
        s_send_up[k : k + 1, :] = shear[dx, pl.ds(order[k], 1), :]

    pl.semaphore_wait(barrier, len(others))

    def s_copy(d):
        src = [s_send_up, shear.at[1], s_send_y.at[0], s_send_y.at[1]][d]
        return remote(src, s_recv.at[d], s_ssem.at[d], s_rsem.at[d], peers[d])

    def exchange_start(copy):
        for d in range(4):
            @pl.when(sends[d])
            def _():
                copy(d).start()

    def exchange_wait(copy):
        for d in range(4):
            @pl.when(has[d])
            def _():
                copy(d).wait_recv()
        for d in range(4):
            @pl.when(sends[d])
            def _():
                copy(d).wait_send()

    exchange_start(s_copy)

    @pl.when(b == 0)
    def _():
        s_recv[0] = shear[1]

    @pl.when(b == nb - 1)
    def _():
        shear[dx + 1] = shear[dx]

    @pl.when(g == 0)
    def _():
        s_recv[2] = s_send_y[1]

    @pl.when(g == ng - 1)
    def _():
        s_recv[3] = s_send_y[0]

    for d in range(4):
        @pl.when(jnp.logical_not(has[d]))
        def _():
            for turn in range(ROUNDS):
                recv[turn, d] = zero_face
            if d < 2:
                fx_recv[d] = jnp.zeros(fx_recv.shape[1:], jnp.float32)

    exchange_wait(s_copy)
    shear[0] = s_recv[0]

    @pl.when(b < nb - 1)
    def _():
        for k in range(dy):
            shear[dx + 1, k : k + 1, :] = s_recv[1, pl.ds(undo[k], 1), :]

    row = lax.broadcasted_iota(jnp.int32, (dy, dz), 0)
    lane = lax.broadcasted_iota(jnp.int32, (dy, dz), 1)

    def y_near(v, low, high):
        ym = jnp.where(row == 0, jnp.broadcast_to(low, v.shape), pltpu.roll(v, 1, 0))
        yp = jnp.where(
            row == dy - 1, jnp.broadcast_to(high, v.shape), pltpu.roll(v, dy - 1, 0)
        )
        return ym, yp

    def z_near(v):
        return pltpu.roll(v, 1, 1), pltpu.roll(v, dz - 1, 1)

    wx[0] = 0.5 * (shear[0] + shear[1])

    def weight_plane(i, best):
        s = shear[i + 1]
        xp = 0.5 * (s + shear[i + 2])
        wx[i + 1] = xp
        xm = 0.5 * (s + shear[i])
        ym, yp = y_near(s, s_recv[2, pl.ds(i, 1), :], s_recv[3, pl.ds(i, 1), :])
        ym = 0.5 * (s + ym)
        yp = 0.5 * (s + yp)
        zm, zp = z_near(s)
        zm = 0.5 * (s + zm)
        zp = 0.5 * (s + zp)
        wyp[i] = yp
        wym[i] = ym
        wzp[i] = jnp.where(lane == dz - 1, 0.0, zp)
        wzm[i] = jnp.where(lane == 0, 0.0, zm)
        total = xp + xm + yp + ym + jnp.where(lane == dz - 1, s, zp) + jnp.where(lane == 0, s, zm)
        bulk = hb[i]
        diagonal = total + 1.5 * bulk
        inv = 1.0 / diagonal
        invd[i] = inv
        dg[i] = total + bulk
        hb[i] = 0.5 * bulk
        for c in range(3):
            d0 = rhs[c, i] * inv
            u[0, c, i + 1] = d0
            y_send[0, 0, c, pl.ds(i, 1), :] = d0[dy - 1 : dy]
            y_send[0, 1, c, pl.ds(i, 1), :] = d0[0:1]
        return jnp.maximum(best, (2.0 * total + 2.5 * bulk) / diagonal)

    best = lax.fori_loop(0, dx, weight_plane, jnp.zeros((dy, dz), jnp.float32), unroll=2)
    m_own[...] = jnp.broadcast_to(jnp.max(best, axis=0, keepdims=True), m_own.shape)

    def h_copy(turn, slot):
        def copy(d):
            src = [
                up_send.at[turn], u.at[slot, :, 1], y_send.at[turn, 0], y_send.at[turn, 1]
            ][d]
            return remote(
                src, recv.at[turn, d], h_ssem.at[turn, d], h_rsem.at[turn, d], peers[d]
            )
        return copy

    def halo_start(turn, slot):
        for c in range(3):
            for k in range(dy):
                up_send[turn, c, k : k + 1, :] = u[slot, c, dx, pl.ds(order[k], 1), :]
        exchange_start(h_copy(turn, slot))

    def halo_wait(turn, slot):
        exchange_wait(h_copy(turn, slot))
        for c in range(3):
            u[slot, c, 0] = recv[turn, 0, c]
            above[c] = recv[turn, 1, c]
        for c in range(3):
            for k in range(dy):
                u[slot, c, dx + 1, k : k + 1, :] = above[c, pl.ds(undo[k], 1), :]

    def apply_plane(i, slot, low, high):
        v = [u[slot, c, i + 1] for c in range(3)]
        coupled = hb[i] * (v[0] + v[1] + v[2])
        out = []
        for c in range(3):
            ym, yp = y_near(v[c], low(c, i), high(c, i))
            zm, zp = z_near(v[c])
            near = wx[i] * u[slot, c, i] + wx[i + 1] * u[slot, c, i + 2]
            near = near + wym[i] * ym + wyp[i] * yp + wzm[i] * zm + wzp[i] * zp
            out.append(dg[i] * v[c] + coupled - near)
        return v, out

    def recv_rows(turn):
        return (
            lambda c, i: recv[turn, 2, c, pl.ds(i, 1), :],
            lambda c, i: recv[turn, 3, c, pl.ds(i, 1), :],
        )

    def bcoef(k):
        return jnp.broadcast_to(coef[k : k + 1, :], (dy, dz))

    def ring_start(own, store, ssem, rsem, peer_of, count, mine):
        copies = []
        for k in range(1, count):
            copies.append(remote(own, store.at[k], ssem.at[k], rsem.at[k], peer_of(k)))
        for copy in copies:
            copy.start()
        return copies

    group_peer = lambda k: (b, lax.rem(g + k, ng))
    brick_peer = lambda k: (lax.rem(b + k, nb), g)

    halo_start(0, 0)
    m_copies = ring_start(m_own, m_all, m_ssem, m_rsem, group_peer, ng, g)
    halo_wait(0, 0)

    low, high = recv_rows(0)

    def first_plane(i, _):
        _, out = apply_plane(i, 0, low, high)
        inv = invd[i]
        for c in range(3):
            r[c, i] = out[c]
            q = out[c] * inv
            u[1, c, i + 1] = q
            y_send[1, 0, c, pl.ds(i, 1), :] = q[dy - 1 : dy]
            y_send[1, 1, c, pl.ds(i, 1), :] = q[0:1]
        return 0

    lax.fori_loop(0, dx, first_plane, 0, unroll=UNROLL)
    halo_start(1, 1)
    top = m_own[...]
    for k, copy in enumerate(m_copies):
        copy.wait()
        top = jnp.maximum(top, m_all[k + 1])
    m2_own[...] = top
    m2_copies = ring_start(m2_own, m2_all, m2_ssem, m2_rsem, brick_peer, nb, b)
    halo_wait(1, 1)
    for k, copy in enumerate(m2_copies):
        copy.wait()
        top = jnp.maximum(top, m2_all[k + 1])
    upper = BOUND_MARGIN * jnp.broadcast_to(jnp.max(top, axis=1, keepdims=True), top.shape)
    lower = LOW_RATIO * upper
    theta = 0.5 * (upper + lower)
    delta = 0.5 * (upper - lower)
    sigma = theta / delta
    damping = 1.0 / sigma
    inv_theta = 1.0 / theta
    coef[0:8] = inv_theta
    rows = []
    for turn in range(1, CHEB):
        following = 1.0 / (2.0 * sigma - damping)
        rows.append((following * damping, 2.0 * following / delta))
        damping = following
    for turn, (a, c2) in enumerate(rows):
        coef[8 + 2 * turn : 9 + 2 * turn] = a[0:1]
        coef[9 + 2 * turn : 10 + 2 * turn] = c2[0:1]
    coef[14:15] = (rows[0][0] * inv_theta + rows[0][1])[0:1]
    coef[15:16] = (rows[0][1] * inv_theta)[0:1]

    alpha, beta, it = bcoef(14), bcoef(15), bcoef(0)

    def combine_plane(i, _):
        for c in range(3):
            d0 = u[0, c, i + 1]
            sol[c, i] = d0 * it
            res[c, i] = rhs[c, i] - r[c, i] * it
            u[0, c, i + 1] = alpha * d0 - beta * u[1, c, i + 1]
        return 0

    lax.fori_loop(0, dx, combine_plane, 0, unroll=UNROLL)
    for c in range(3):
        for p in (0, dx + 1):
            u[0, c, p] = alpha * u[0, c, p] - beta * u[1, c, p]
        for d in (2, 3):
            recv[1, d, c] = alpha[:dx] * recv[0, d, c] - beta[:dx] * recv[1, d, c]

    def step(slot, low, high, a, c2, following):
        other = 1 - slot

        def plane(i, sums):
            v, out = apply_plane(i, slot, low, high)
            inv = invd[i]
            new = []
            for c in range(3):
                rest = res[c, i] - out[c]
                res[c, i] = rest
                sol[c, i] = sol[c, i] + v[c]
                if following is None:
                    new.append(sums[c] + rest)
                    continue
                ahead = c2 * (rest * inv)
                if a is not None:
                    ahead = ahead + a * v[c]
                u[other, c, i + 1] = ahead
                y_send[following, 0, c, pl.ds(i, 1), :] = ahead[dy - 1 : dy]
                y_send[following, 1, c, pl.ds(i, 1), :] = ahead[0:1]
            return tuple(new)

        init = ()
        if following is None:
            init = tuple(jnp.zeros((dy, dz), jnp.float32) for _ in range(3))
        return lax.fori_loop(0, dx, plane, init, unroll=UNROLL)

    slot = 0
    for turn in range(1, CHEB):
        low, high = recv_rows(turn)
        if turn + 1 < CHEB:
            step(slot, low, high, bcoef(8 + 2 * turn), bcoef(9 + 2 * turn), turn + 1)
            slot = 1 - slot
            halo_start(turn + 1, slot)
            halo_wait(turn + 1, slot)
        else:
            sums = step(slot, low, high, None, None, None)

    c_own[...] = jnp.zeros(c_own.shape, jnp.float32)
    for c in range(3):
        c_own[c : c + 1, :] = jnp.sum(sums[c], axis=0, keepdims=True)
    c_all[g] = c_own[...]
    c_copies = [
        remote(c_own, c_all.at[g], c_ssem.at[k], c_rsem.at[k], group_peer(k))
        for k in range(1, ng)
    ]
    for copy in c_copies:
        copy.start()
    for k in range(1, ng):
        source = lax.rem(g + ng - k, ng)
        remote(c_own, c_all.at[source], c_ssem.at[k], c_rsem.at[k], group_peer(k)).wait()
    cells_z = dz // BLOCK_Z
    size = 3 * cells_z * ng
    flat = c_all[...].reshape(ng * 8, dz)
    li = lax.broadcasted_iota(jnp.int32, (dz, size), 0)
    ki = lax.broadcasted_iota(jnp.int32, (dz, size), 1)
    gather = jnp.where(li // BLOCK_Z == ki % cells_z, 1.0 / (dx * dy * BLOCK_Z), 0.0)
    spread = jnp.dot(flat, gather, precision=HIGHEST, preferred_element_type=jnp.float32)
    ri = lax.broadcasted_iota(jnp.int32, (ng * 8, size), 0)
    kk = lax.broadcasted_iota(jnp.int32, (ng * 8, size), 1) // cells_z
    mine = (ri // 8 == kk // 3) & (ri % 8 == kk % 3)
    vector = jnp.sum(jnp.where(mine, spread, 0.0), axis=0, keepdims=True)
    correction = jnp.sum(inverse[0] * vector, axis=1, keepdims=True)
    bi = lax.broadcasted_iota(jnp.int32, (size, dz), 0)
    bl = lax.broadcasted_iota(jnp.int32, (size, dz), 1)
    table = jnp.where(bi % cells_z == bl // BLOCK_Z, jnp.broadcast_to(correction, (size, dz)), 0.0)
    f_all[...] = jnp.zeros(f_all.shape, jnp.float32)
    for k in range(ng):
        for c in range(3):
            start = (k * 3 + c) * cells_z
            f_all[k + 1, c : c + 1, :] = jnp.sum(
                table[start : start + cells_z], axis=0, keepdims=True
            )
    fx_own[...] = f_all[g + 1]

    def f_copy(d):
        return remote(fx_own, fx_recv.at[d], f_ssem.at[d], f_rsem.at[d], peers[d])

    for d in range(2):
        @pl.when(sends[d])
        def _():
            f_copy(d).start()

    slot = 0

    def fill_plane(i, _):
        for c in range(3):
            u[0, c, i + 1] = jnp.broadcast_to(fx_own[c : c + 1, :], (dy, dz))
        return 0

    lax.fori_loop(0, dx, fill_plane, 0, unroll=UNROLL)
    for d in range(2):
        @pl.when(has[d])
        def _():
            f_copy(d).wait_recv()
        @pl.when(sends[d])
        def _():
            f_copy(d).wait_send()
    for c in range(3):
        u[0, c, 0] = jnp.broadcast_to(fx_recv[0, c : c + 1, :], (dy, dz))
        u[0, c, dx + 1] = jnp.broadcast_to(fx_recv[1, c : c + 1, :], (dy, dz))
    step(
        0,
        lambda c, i: f_all[g, c : c + 1, :],
        lambda c, i: f_all[g + 2, c : c + 1, :],
        None,
        bcoef(0),
        CHEB,
    )
    slot = 1
    for turn in range(CHEB):
        halo_start(CHEB + turn, slot)
        halo_wait(CHEB + turn, slot)
        low, high = recv_rows(CHEB + turn)
        if turn + 1 < CHEB:
            step(slot, low, high, bcoef(8 + 2 * turn), bcoef(9 + 2 * turn), CHEB + turn + 1)
            slot = 1 - slot
        else:
            step(slot, low, high, None, None, None)


def per_device(rhs, material, level, mortar, mu, lam, inverse):
    nb = lax.axis_size("bricks")
    ng = lax.axis_size("group")
    dx, dy, dz = material.shape
    f32 = jnp.float32
    vmem = pl.BlockSpec(memory_space=pltpu.VMEM)
    smem = pl.BlockSpec(memory_space=pltpu.SMEM)
    dma = pltpu.SemaphoreType.DMA
    grid = pltpu.VMEM((dx, dy, dz), f32)
    scratch = [
        pltpu.VMEM((2, 3, dx + 2, dy, dz), f32),
        pltpu.VMEM((3, dx, dy, dz), f32),
        pltpu.VMEM((dx + 2, dy, dz), f32),
        pltpu.VMEM((dx + 1, dy, dz), f32),
        grid, grid, grid, grid, grid, grid, grid,
        pltpu.VMEM((16, dz), f32),
        pltpu.SMEM((dy,), jnp.int32),
        pltpu.VMEM((dy, dz), f32),
        pltpu.VMEM((2, dx, dz), f32),
        pltpu.VMEM((4, dx, dz), f32),
        pltpu.VMEM((3, dy, dz), f32),
        pltpu.VMEM((ROUNDS, 3, dy, dz), f32),
        pltpu.VMEM((ROUNDS, 2, 3, dx, dz), f32),
        pltpu.VMEM((ROUNDS, 4, 3, dx, dz), f32),
        pltpu.VMEM((8, dz), f32),
        pltpu.VMEM((ng, 8, dz), f32),
        pltpu.VMEM((8, dz), f32),
        pltpu.VMEM((nb, 8, dz), f32),
        pltpu.VMEM((8, dz), f32),
        pltpu.VMEM((ng, 8, dz), f32),
        pltpu.VMEM((ng + 2, 8, dz), f32),
        pltpu.VMEM((8, dz), f32),
        pltpu.VMEM((2, 8, dz), f32),
        dma((4,)), dma((4,)),
        dma((ROUNDS, 4)), dma((ROUNDS, 4)),
        dma((ng,)), dma((ng,)),
        dma((nb,)), dma((nb,)),
        dma((ng,)), dma((ng,)),
        dma((2,)), dma((2,)),
    ]
    return pl.pallas_call(
        functools.partial(kernel, nb, ng, dx, dy, dz),
        out_shape=(
            jax.ShapeDtypeStruct(rhs.shape, f32),
            jax.ShapeDtypeStruct(rhs.shape, f32),
        ),
        in_specs=[vmem, vmem, smem, smem, smem, smem, vmem],
        out_specs=(vmem, vmem),
        scratch_shapes=scratch,
        compiler_params=pltpu.CompilerParams(collective_id=0, has_side_effects=True),
    )(rhs, material, level, mortar, mu, lam, inverse)


def solution(mesh):
    return jax.shard_map(
        per_device,
        mesh=mesh,
        in_specs=(
            P(None, "bricks", "group", None),
            P("bricks", "group", None),
            P("bricks", "group"),
            P("bricks", "group", None),
            P(),
            P(),
            P("bricks", None, None),
        ),
        out_specs=(P(None, "bricks", "group", None), P(None, "bricks", "group", None)),
        check_vma=False,
    )
```

time: 273 us -> 54.4 us (0.20); the launches traced: 269 us -> 54.3 us
  starting transfers between devices: 116 us -> 0 us
  Pallas kernels: 0 us -> 50.4 us
  blocking collectives: 49.7 us -> 0 us
  local copies, waits for them, and re-layouts: 51.2 us -> 2.57 us
  other arithmetic: 47.3 us -> 0 us
  between operations: 4.28 us -> 1.29 us
    ppermute x40 -> x0, starting transfers between devices: 116 us -> none  [the longest x20 65.9 us: shifted(): return lax.ppermute(block, axis, route)]
    pallas_call x0 -> x1, Pallas kernels: none -> 50.4 us  [per_device(): pl.pallas_call(functools.partial(kernel, nb, ng, dx, dy, dz), out_shape=(...]
    pmax x1 -> x0, blocking collectives: 42.2 us -> none  [per_device(): upper = bound_margin * lax.pmax(jnp.max(bound_ratio), ('bricks', 'group'))]
    reduce_sum x11 -> x0, other arithmetic: 29.3 us -> none  [the longest x9 25.9 us: apply(): coupled = jnp.sum(field, axis=0)]
    slice x32 -> x0, local copies, waits for them, and re-layouts: 23.1 us -> none  [the longest x9 10.5 us: neighbours(): z_plus = jnp.pad(field[:, :, :, 1:], ((0, 0), (0, 0), (0, 0), (0, 1)))]
    scatter x10 -> x0, local copies, waits for them, and re-layouts: 10.3 us -> none  [neighbours(): above = jnp.zeros_like(received).at[:, order].set(received)]
    psum x1 -> x0, blocking collectives: 7.51 us -> none  [per_device(): whole = lax.psum(padded, 'group')]
    unnamed x76 -> x4, local copies, waits for them, and re-layouts: 9.03 us -> 2.57 us
  transfers between devices with their start and end apart: 40 -> 0, of which waited for: 1 -> 0; matrix products, arithmetic and copies ran while one was open for 9% -> 0% of each run, Pallas kernels for 0% -> 0%
where the time goes in v1:
time: 54.4 us; the launch traced here: 54.3 us
  Pallas kernels  50.4 us (93%)
  local copies, waits for them, and re-layouts  2.57 us (5%)
  between operations  1.29 us (2%)
    pallas_call x1, Pallas kernels, per_device(): pl.pallas_call(functools.partial(kernel, nb, ng, dx, dy, dz), out_shape=(...  50.4 us
    unnamed x4, local copies, waits for them, and re-layouts  2.57 us

profile of v1, /device:TPU:0, one launch (start us, length us, event | category | flops | bytes accessed | tf_op | source)
XLA Modules:
  0.0 54.3 jit_solution(5833193215661128978)
XLA Ops:
  1.3 50.4 %shard_map.86 = (f32[3,16,16,128]{3,2,1,0:T(8,128)}, f32[3,16,16,128]{3,2,1,0:T(8,128)}) custom-call(f32[3,16,16,128]{3,2,1,0:T(8,128)} %rhs.1, s32[16,16,128]{2,1,0:T(8,128)} %material.1, s32[1,1]{1,0:T(1,128)S(6)} %copy.11.level, s32[1,1,16]{2,1,0:T(1,128)} %mortar.1, f32[4]{0:T(128)} %mu.1, f32[4]{0:T(128)} %lam.1, f32[1,48,48]{2,1,0:T(8,128)} %inverse.1), custom_call_target="tpu_custom_call" | custom-call | tf_op jit(solution)/shard_map/pallas_call | solution.py:464
  51.7 0.0 copy-start
  51.7 1.8 %copy.12 = f32[3,16,16,128]{3,2,1,0:T(8,128)} copy(f32[3,16,16,128]{3,2,1,0:T(8,128)} %get-tuple-element.4) | data formatting | bytes 786432
  53.5 0.0 copy-done
  53.5 0.7 %copy.13 = f32[3,16,16,128]{3,2,1,0:T(8,128)} copy(f32[3,16,16,128]{3,2,1,0:T(8,128)S(1)} %copy-done) | data formatting | bytes 786432
Async XLA Ops:
  51.7 1.8 %copy-start = (f32[3,16,16,128]{3,2,1,0:T(8,128)S(1)}, f32[3,16,16,128]{3,2,1,0:T(8,128)}, u32[]{:S(2)}) copy-start(f32[3,16,16,128]{3,2,1,0:T(8,128)} %get-tuple-element.5) | copy-start | bytes 1179652

commit v2 on v1

--- a/solution.py
+++ b/solution.py
@@ -13,6 +13,7 @@
 BOUND_MARGIN = 1.1
 ROUNDS = 2 * CHEB
 UNROLL = 4
+SWEEP = 7
 HIGHEST = lax.Precision.HIGHEST
 
 
@@ -46,7 +47,8 @@
             barrier, inc=1, device_id=peer, device_id_type=pl.DeviceIdType.MESH
         )
 
-    scale = jnp.where(level[0, 0] == 0, 1.0, jnp.where(level[0, 0] == 1, 4.0, 16.0))
+    grade = jnp.broadcast_to(level[...], (dy, dz))
+    scale = jnp.where(grade == 0, 1.0, jnp.where(grade == 1, 4.0, 16.0))
     zero_face = jnp.zeros((3, dx, dz), jnp.float32)
 
     order = [mortar[0, 0, k] for k in range(dy)]
@@ -57,10 +59,10 @@
         undo[k] = total
 
     def lookup(ids, table):
-        total = jnp.where(ids == 0, table[0] * scale, 0.0)
+        total = jnp.where(ids == 0, table[0], 0.0)
         for entry in range(1, 4):
-            total = jnp.where(ids == entry, table[entry] * scale, total)
-        return total
+            total = jnp.where(ids == entry, table[entry], total)
+        return total * scale
 
     def shear_plane(i, _):
         ids = material[i]
@@ -81,8 +83,8 @@
         src = [s_send_up, shear.at[1], s_send_y.at[0], s_send_y.at[1]][d]
         return remote(src, s_recv.at[d], s_ssem.at[d], s_rsem.at[d], peers[d])
 
-    def exchange_start(copy):
-        for d in range(4):
+    def exchange_start(copy, directions=(0, 1, 2, 3)):
+        for d in directions:
             @pl.when(sends[d])
             def _():
                 copy(d).start()
@@ -144,7 +146,31 @@
     def z_near(v):
         return pltpu.roll(v, 1, 1), pltpu.roll(v, dz - 1, 1)
 
+    def h_copy(turn, slot):
+        def copy(d):
+            src = [
+                up_send.at[turn], u.at[slot, :, 1], y_send.at[turn, 0], y_send.at[turn, 1]
+            ][d]
+            return remote(
+                src, recv.at[turn, d], h_ssem.at[turn, d], h_rsem.at[turn, d], peers[d]
+            )
+        return copy
+
+    def sweep(plane, turn, slot, carry, unroll):
+        carry = plane(0, carry)
+        carry = plane(dx - 1, carry)
+        if turn is not None:
+            for c in range(3):
+                for k in range(dy):
+                    up_send[turn, c, k : k + 1, :] = u[slot, c, dx, pl.ds(order[k], 1), :]
+            exchange_start(h_copy(turn, slot), (0, 1))
+        carry = lax.fori_loop(1, dx - 1, plane, carry, unroll=unroll)
+        if turn is not None:
+            exchange_start(h_copy(turn, slot), (2, 3))
+        return carry
+
     wx[0] = 0.5 * (shear[0] + shear[1])
+    wx[dx] = 0.5 * (shear[dx] + shear[dx + 1])
 
     def weight_plane(i, best):
         s = shear[i + 1]
@@ -175,24 +201,8 @@
             y_send[0, 1, c, pl.ds(i, 1), :] = d0[0:1]
         return jnp.maximum(best, (2.0 * total + 2.5 * bulk) / diagonal)
 
-    best = lax.fori_loop(0, dx, weight_plane, jnp.zeros((dy, dz), jnp.float32), unroll=2)
+    best = sweep(weight_plane, 0, 0, jnp.zeros((dy, dz), jnp.float32), 2)
     m_own[...] = jnp.broadcast_to(jnp.max(best, axis=0, keepdims=True), m_own.shape)
-
-    def h_copy(turn, slot):
-        def copy(d):
-            src = [
-                up_send.at[turn], u.at[slot, :, 1], y_send.at[turn, 0], y_send.at[turn, 1]
-            ][d]
-            return remote(
-                src, recv.at[turn, d], h_ssem.at[turn, d], h_rsem.at[turn, d], peers[d]
-            )
-        return copy
-
-    def halo_start(turn, slot):
-        for c in range(3):
-            for k in range(dy):
-                up_send[turn, c, k : k + 1, :] = u[slot, c, dx, pl.ds(order[k], 1), :]
-        exchange_start(h_copy(turn, slot))
 
     def halo_wait(turn, slot):
         exchange_wait(h_copy(turn, slot))
@@ -235,7 +245,6 @@
     group_peer = lambda k: (b, lax.rem(g + k, ng))
     brick_peer = lambda k: (lax.rem(b + k, nb), g)
 
-    halo_start(0, 0)
     m_copies = ring_start(m_own, m_all, m_ssem, m_rsem, group_peer, ng, g)
     halo_wait(0, 0)
 
@@ -252,8 +261,7 @@
             y_send[1, 1, c, pl.ds(i, 1), :] = q[0:1]
         return 0
 
-    lax.fori_loop(0, dx, first_plane, 0, unroll=UNROLL)
-    halo_start(1, 1)
+    sweep(first_plane, 1, 1, 0, SWEEP)
     top = m_own[...]
     for k, copy in enumerate(m_copies):
         copy.wait()
@@ -325,7 +333,7 @@
         init = ()
         if following is None:
             init = tuple(jnp.zeros((dy, dz), jnp.float32) for _ in range(3))
-        return lax.fori_loop(0, dx, plane, init, unroll=UNROLL)
+        return sweep(plane, following, other, init, SWEEP)
 
     slot = 0
     for turn in range(1, CHEB):
@@ -333,7 +341,6 @@
         if turn + 1 < CHEB:
             step(slot, low, high, bcoef(8 + 2 * turn), bcoef(9 + 2 * turn), turn + 1)
             slot = 1 - slot
-            halo_start(turn + 1, slot)
             halo_wait(turn + 1, slot)
         else:
             sums = step(slot, low, high, None, None, None)
@@ -411,7 +418,6 @@
     )
     slot = 1
     for turn in range(CHEB):
-        halo_start(CHEB + turn, slot)
         halo_wait(CHEB + turn, slot)
         low, high = recv_rows(CHEB + turn)
         if turn + 1 < CHEB:
@@ -467,10 +473,12 @@
             jax.ShapeDtypeStruct(rhs.shape, f32),
             jax.ShapeDtypeStruct(rhs.shape, f32),
         ),
-        in_specs=[vmem, vmem, smem, smem, smem, smem, vmem],
+        in_specs=[vmem, vmem, vmem, smem, smem, smem, vmem],
         out_specs=(vmem, vmem),
         scratch_shapes=scratch,
-        compiler_params=pltpu.CompilerParams(collective_id=0, has_side_effects=True),
+        compiler_params=pltpu.CompilerParams(
+            collective_id=0, has_side_effects=True, vmem_limit_bytes=16 * 2**20
+        ),
     )(rhs, material, level, mortar, mu, lam, inverse)
 
 

time: 54.4 us -> 50.9 us (0.936)
  Pallas kernels: 50.4 us -> 45.2 us
  local copies, waits for them, and re-layouts: 2.57 us -> 4.14 us
    pallas_call x1, Pallas kernels: 50.4 us -> 45.2 us  [per_device(): pl.pallas_call(functools.partial(kernel, nb, ng, dx, dy, dz), out_shape=(...]
    unnamed x4 -> x14, local copies, waits for them, and re-layouts: 2.57 us -> 4.14 us
where the time goes in v2:
time: 50.9 us; the launch traced here: 50.7 us
  Pallas kernels  45.2 us (89%)
  local copies, waits for them, and re-layouts  4.14 us (8%)
  between operations  1.37 us (3%)
    pallas_call x1, Pallas kernels, per_device(): pl.pallas_call(functools.partial(kernel, nb, ng, dx, dy, dz), out_shape=(...  45.2 us
    unnamed x14, local copies, waits for them, and re-layouts  4.14 us

profile of v2, /device:TPU:0, one launch (start us, length us, event | category | flops | bytes accessed | tf_op | source)
XLA Modules:
  0.0 50.7 jit_solution(7655091112474806234)
XLA Ops:
  0.6 0.0 copy-start.5
  0.6 0.0 copy-start.4
  0.7 0.0 copy-start.3
  1.3 0.0 copy-done.5
  1.3 0.0 copy-done.4
  1.4 0.0 copy-done.3
  1.4 0.0 copy-start
  1.4 1.0 %copy-done = f32[3,16,16,128]{3,2,1,0:T(8,128)S(1)} copy-done((f32[3,16,16,128]{3,2,1,0:T(8,128)S(1)}, f32[3,16,16,128]{3,2,1,0:T(8,128)}, u32[]{:S(2)}) %copy-start) | copy-done | bytes 393240
  2.4 0.0 copy-start.1
  2.4 0.9 %copy-done.1 = s32[16,16,128]{2,1,0:T(8,128)S(1)} copy-done((s32[16,16,128]{2,1,0:T(8,128)S(1)}, s32[16,16,128]{2,1,0:T(8,128)}, u32[]{:S(2)}) %copy-start.1) | copy-done | bytes 131096
  3.3 0.0 copy-start.2
  3.3 0.7 %copy-done.2 = f32[1,48,48]{2,1,0:T(8,128)S(1)} copy-done((f32[1,48,48]{2,1,0:T(8,128)S(1)}, f32[1,48,48]{2,1,0:T(8,128)}, u32[]{:S(2)}) %copy-start.2) | copy-done | bytes 9240
  4.0 45.2 %shard_map.86 = (f32[3,16,16,128]{3,2,1,0:T(8,128)S(1)}, f32[3,16,16,128]{3,2,1,0:T(8,128)S(1)}) custom-call(f32[3,16,16,128]{3,2,1,0:T(8,128)S(1)} %copy-done, s32[16,16,128]{2,1,0:T(8,128)S(1)} %copy-done.1, s32[1,1]{1,0:T(1,128)S(6)} %copy.11.level, s32[1,1,16]{2,1,0:T(1,128)S(1)} %copy-done.3, f32[4]{0:T(128)S(1)} %copy-done.4, f32[4]{0:T(128)S(1)} %copy-done.5, ...), custom_call_target="tpu_custom_call" | custom-call | tf_op jit(solution)/shard_map/pallas_call | solution.py:470
  49.2 0.7 %copy.12 = f32[3,16,16,128]{3,2,1,0:T(8,128)} copy(f32[3,16,16,128]{3,2,1,0:T(8,128)S(1)} %get-tuple-element.4) | data formatting | bytes 786432
  49.9 0.7 %copy.13 = f32[3,16,16,128]{3,2,1,0:T(8,128)} copy(f32[3,16,16,128]{3,2,1,0:T(8,128)S(1)} %get-tuple-element.5) | data formatting | bytes 786432
Async XLA Ops:
  0.6 0.7 %copy-start.5 = (f32[4]{0:T(128)S(1)}, f32[4]{0:T(128)}, u32[]{:S(2)}) copy-start(f32[4]{0:T(128)} %lam.1) | copy-start | bytes 52
  0.6 0.7 %copy-start.4 = (f32[4]{0:T(128)S(1)}, f32[4]{0:T(128)}, u32[]{:S(2)}) copy-start(f32[4]{0:T(128)} %mu.1) | copy-start | bytes 52
  0.7 0.7 %copy-start.3 = (s32[1,1,16]{2,1,0:T(1,128)S(1)}, s32[1,1,16]{2,1,0:T(1,128)}, u32[]{:S(2)}) copy-start(s32[1,1,16]{2,1,0:T(1,128)} %mortar.1) | copy-start | bytes 196
  1.4 1.0 %copy-start = (f32[3,16,16,128]{3,2,1,0:T(8,128)S(1)}, f32[3,16,16,128]{3,2,1,0:T(8,128)}, u32[]{:S(2)}) copy-start(f32[3,16,16,128]{3,2,1,0:T(8,128)} %rhs.1) | copy-start | bytes 1179652
  2.4 0.9 %copy-start.1 = (s32[16,16,128]{2,1,0:T(8,128)S(1)}, s32[16,16,128]{2,1,0:T(8,128)}, u32[]{:S(2)}) copy-start(s32[16,16,128]{2,1,0:T(8,128)} %material.1) | copy-start | bytes 393220
  3.3 0.7 %copy-start.2 = (f32[1,48,48]{2,1,0:T(8,128)S(1)}, f32[1,48,48]{2,1,0:T(8,128)}, u32[]{:S(2)}) copy-start(f32[1,48,48]{2,1,0:T(8,128)} %inverse.1) | copy-start | bytes 27652

commit v3 on v2

--- a/solution.py
+++ b/solution.py
@@ -19,13 +19,13 @@
 
 def kernel(
     nb, ng, dx, dy, dz,
-    rhs, material, level, mortar, mu, lam, inverse,
-    sol, res,
+    rhs_in, material_in, level, mortar, mu, lam, inverse_in,
+    sol, res, rhs, material, inverse,
     u, r, shear, wx, wyp, wym, wzp, wzm, dg, hb, invd, coef, undo,
     s_send_up, s_send_y, s_recv, above, up_send, y_send, recv,
-    m_own, m_all, m2_own, m2_all, c_own, c_all, f_all, fx_own, fx_recv,
+    m_own, m_all, m2_own, m2_all, c_own, c_all, f_all, inv_recv, pack_send, pack_top, pack_recv, in_sem,
     s_ssem, s_rsem, h_ssem, h_rsem,
-    m_ssem, m_rsem, m2_ssem, m2_rsem, c_ssem, c_rsem, f_ssem, f_rsem,
+    m_ssem, m_rsem, m2_ssem, m2_rsem, c_ssem, c_rsem, p_ssem, p_rsem, i_ssem, i_rsem,
 ):
     b = lax.axis_index("bricks")
     g = lax.axis_index("group")
@@ -42,10 +42,26 @@
     barrier = pltpu.get_barrier_semaphore()
     others = [(b, lax.rem(g + k, ng)) for k in range(1, ng)]
     others += [(lax.rem(b + k, nb), g) for k in range(1, nb)]
+    around = [(lax.rem(g + k, ng)) for k in range(1, ng)]
     for peer in others:
         pl.semaphore_signal(
             barrier, inc=1, device_id=peer, device_id_type=pl.DeviceIdType.MESH
         )
+    for d in range(2):
+        @pl.when(has[d])
+        def _():
+            for at in around:
+                pl.semaphore_signal(
+                    barrier, inc=1, device_id=(b - 1 + 2 * d, at),
+                    device_id_type=pl.DeviceIdType.MESH,
+                )
+
+    def fetch(k):
+        source = [material_in, rhs_in, inverse_in.at[0]][k]
+        return pltpu.make_async_copy(source, [material, rhs, inverse][k], in_sem.at[k])
+
+    for k in range(3):
+        fetch(k).start()
 
     grade = jnp.broadcast_to(level[...], (dy, dz))
     scale = jnp.where(grade == 0, 1.0, jnp.where(grade == 1, 4.0, 16.0))
@@ -73,11 +89,14 @@
         s_send_y[1, pl.ds(i, 1), :] = plane[0:1]
         return 0
 
+    for k in range(3):
+        fetch(k).wait()
     lax.fori_loop(0, dx, shear_plane, 0, unroll=UNROLL)
     for k in range(dy):
         s_send_up[k : k + 1, :] = shear[dx, pl.ds(order[k], 1), :]
 
-    pl.semaphore_wait(barrier, len(others))
+    both = jnp.where(has[0], len(around), 0) + jnp.where(has[1], len(around), 0)
+    pl.semaphore_wait(barrier, len(others) + both)
 
     def s_copy(d):
         src = [s_send_up, shear.at[1], s_send_y.at[0], s_send_y.at[1]][d]
@@ -89,12 +108,12 @@
             def _():
                 copy(d).start()
 
-    def exchange_wait(copy):
-        for d in range(4):
+    def exchange_wait(copy, directions=(0, 1, 2, 3)):
+        for d in directions:
             @pl.when(has[d])
             def _():
                 copy(d).wait_recv()
-        for d in range(4):
+        for d in directions:
             @pl.when(sends[d])
             def _():
                 copy(d).wait_send()
@@ -108,6 +127,7 @@
     @pl.when(b == nb - 1)
     def _():
         shear[dx + 1] = shear[dx]
+        s_recv[1] = shear[dx]
 
     @pl.when(g == 0)
     def _():
@@ -122,8 +142,10 @@
         def _():
             for turn in range(ROUNDS):
                 recv[turn, d] = zero_face
+            pack_recv[d] = jnp.zeros(pack_recv.shape[1:], jnp.float32)
             if d < 2:
-                fx_recv[d] = jnp.zeros(fx_recv.shape[1:], jnp.float32)
+                inv_recv[d] = jnp.zeros(inv_recv.shape[1:], jnp.float32)
+                c_all[2 * d] = jnp.zeros(c_all.shape[1:], jnp.float32)
 
     exchange_wait(s_copy)
     shear[0] = s_recv[0]
@@ -193,7 +215,22 @@
         inv = 1.0 / diagonal
         invd[i] = inv
         dg[i] = total + bulk
-        hb[i] = 0.5 * bulk
+        half = 0.5 * bulk
+        hb[i] = half
+        none = jnp.zeros((1, dz), jnp.float32)
+        for d, y in ((2, dy - 1), (3, 0)):
+            pack_send[d, 0, pl.ds(i, 1), :] = inv[y : y + 1]
+            pack_send[d, 1, pl.ds(i, 1), :] = half[y : y + 1]
+            first, last = isinstance(i, int) and i == 0, isinstance(i, int) and i == dx - 1
+            pack_send[d, 2, pl.ds(i, 1), :] = xm[y : y + 1] if first else none
+            pack_send[d, 3, pl.ds(i, 1), :] = xp[y : y + 1] if last else none
+        if isinstance(i, int):
+            planes = (inv, half, jnp.where(row == 0, ym, 0.0), jnp.where(row == dy - 1, yp, 0.0))
+            for k, value in enumerate(planes):
+                if i == 0:
+                    pack_send[1, k] = value
+                else:
+                    pack_top[k] = value
         for c in range(3):
             d0 = rhs[c, i] * inv
             u[0, c, i + 1] = d0
@@ -206,6 +243,9 @@
 
     def halo_wait(turn, slot):
         exchange_wait(h_copy(turn, slot))
+        place_halo(turn, slot)
+
+    def place_halo(turn, slot):
         for c in range(3):
             u[slot, c, 0] = recv[turn, 0, c]
             above[c] = recv[turn, 1, c]
@@ -262,12 +302,22 @@
         return 0
 
     sweep(first_plane, 1, 1, 0, SWEEP)
+
+    def p_copy(d):
+        return remote(
+            pack_send.at[d], pack_recv.at[d], p_ssem.at[d], p_rsem.at[d], peers[d]
+        )
+
+    for q in range(4):
+        for k in range(dy):
+            pack_send[0, q, k : k + 1, :] = pack_top[q, pl.ds(order[k], 1), :]
     top = m_own[...]
     for k, copy in enumerate(m_copies):
         copy.wait()
         top = jnp.maximum(top, m_all[k + 1])
     m2_own[...] = top
     m2_copies = ring_start(m2_own, m2_all, m2_ssem, m2_rsem, brick_peer, nb, b)
+    exchange_start(p_copy)
     halo_wait(1, 1)
     for k, copy in enumerate(m2_copies):
         copy.wait()
@@ -308,7 +358,7 @@
         for d in (2, 3):
             recv[1, d, c] = alpha[:dx] * recv[0, d, c] - beta[:dx] * recv[1, d, c]
 
-    def step(slot, low, high, a, c2, following):
+    def step(slot, low, high, a, c2, following, summed=False, send=True):
         other = 1 - slot
 
         def plane(i, sums):
@@ -319,21 +369,27 @@
                 rest = res[c, i] - out[c]
                 res[c, i] = rest
                 sol[c, i] = sol[c, i] + v[c]
+                if summed:
+                    new.append(sums[c] + rest)
                 if following is None:
-                    new.append(sums[c] + rest)
                     continue
                 ahead = c2 * (rest * inv)
                 if a is not None:
                     ahead = ahead + a * v[c]
                 u[other, c, i + 1] = ahead
+                if not send:
+                    continue
                 y_send[following, 0, c, pl.ds(i, 1), :] = ahead[dy - 1 : dy]
                 y_send[following, 1, c, pl.ds(i, 1), :] = ahead[0:1]
             return tuple(new)
 
         init = ()
-        if following is None:
+        if summed:
             init = tuple(jnp.zeros((dy, dz), jnp.float32) for _ in range(3))
-        return sweep(plane, following, other, init, SWEEP)
+        return sweep(plane, following if send else None, other, init, SWEEP)
+
+    def i_copy(d):
+        return remote(inverse, inv_recv.at[d], i_ssem.at[d], i_rsem.at[d], peers[d])
 
     slot = 0
     for turn in range(1, CHEB):
@@ -341,26 +397,55 @@
         if turn + 1 < CHEB:
             step(slot, low, high, bcoef(8 + 2 * turn), bcoef(9 + 2 * turn), turn + 1)
             slot = 1 - slot
+            if turn == 1:
+                exchange_start(i_copy, (0, 1))
             halo_wait(turn + 1, slot)
         else:
-            sums = step(slot, low, high, None, None, None)
+            sums = step(slot, low, high, None, bcoef(0), CHEB, summed=True)
 
     c_own[...] = jnp.zeros(c_own.shape, jnp.float32)
     for c in range(3):
         c_own[c : c + 1, :] = jnp.sum(sums[c], axis=0, keepdims=True)
-    c_all[g] = c_own[...]
-    c_copies = [
-        remote(c_own, c_all.at[g], c_ssem.at[k], c_rsem.at[k], group_peer(k))
-        for k in range(1, ng)
-    ]
-    for copy in c_copies:
-        copy.start()
-    for k in range(1, ng):
+    c_all[1, g] = c_own[...]
+
+    def c_copy(q, k):
+        slot = q * ng + k
+        return remote(
+            c_own, c_all.at[q, g], c_ssem.at[slot], c_rsem.at[slot],
+            (b + 1 - q, lax.rem(g + k, ng)),
+        )
+
+    def c_arrival(q, k):
+        slot = q * ng + k
         source = lax.rem(g + ng - k, ng)
-        remote(c_own, c_all.at[source], c_ssem.at[k], c_rsem.at[k], group_peer(k)).wait()
+        return remote(
+            c_own, c_all.at[q, source], c_ssem.at[slot], c_rsem.at[slot],
+            (b + 1 - q, lax.rem(g + k, ng)),
+        )
+
+    def coarse_all(to_do, flags):
+        for q in (0, 2, 1):
+            first = 1 if q == 1 else 0
+            if q == 1:
+                for k in range(first, ng):
+                    to_do(q, k)
+                continue
+
+            @pl.when(flags[q])
+            def _():
+                for k in range(first, ng):
+                    to_do(q, k)
+
+    coarse_all(lambda q, k: c_copy(q, k).start(), {0: has[1], 2: has[0]})
+    f_all[...] = jnp.zeros(f_all.shape, jnp.float32)
+    exchange_wait(p_copy)
+    exchange_wait(i_copy, (0, 1))
+    coarse_all(lambda q, k: c_arrival(q, k).wait_recv(), {0: has[0], 2: has[1]})
+    coarse_all(lambda q, k: c_copy(q, k).wait_send(), {0: has[1], 2: has[0]})
+
     cells_z = dz // BLOCK_Z
     size = 3 * cells_z * ng
-    flat = c_all[...].reshape(ng * 8, dz)
+    flat = c_all[...].reshape(3 * ng * 8, dz)
     li = lax.broadcasted_iota(jnp.int32, (dz, size), 0)
     ki = lax.broadcasted_iota(jnp.int32, (dz, size), 1)
     gather = jnp.where(li // BLOCK_Z == ki % cells_z, 1.0 / (dx * dy * BLOCK_Z), 0.0)
@@ -368,57 +453,74 @@
     ri = lax.broadcasted_iota(jnp.int32, (ng * 8, size), 0)
     kk = lax.broadcasted_iota(jnp.int32, (ng * 8, size), 1) // cells_z
     mine = (ri // 8 == kk // 3) & (ri % 8 == kk % 3)
-    vector = jnp.sum(jnp.where(mine, spread, 0.0), axis=0, keepdims=True)
-    correction = jnp.sum(inverse[0] * vector, axis=1, keepdims=True)
     bi = lax.broadcasted_iota(jnp.int32, (size, dz), 0)
     bl = lax.broadcasted_iota(jnp.int32, (size, dz), 1)
-    table = jnp.where(bi % cells_z == bl // BLOCK_Z, jnp.broadcast_to(correction, (size, dz)), 0.0)
-    f_all[...] = jnp.zeros(f_all.shape, jnp.float32)
-    for k in range(ng):
-        for c in range(3):
-            start = (k * 3 + c) * cells_z
-            f_all[k + 1, c : c + 1, :] = jnp.sum(
-                table[start : start + cells_z], axis=0, keepdims=True
-            )
-    fx_own[...] = f_all[g + 1]
-
-    def f_copy(d):
-        return remote(fx_own, fx_recv.at[d], f_ssem.at[d], f_rsem.at[d], peers[d])
-
-    for d in range(2):
-        @pl.when(sends[d])
-        def _():
-            f_copy(d).start()
-
-    slot = 0
+    placed = bi % cells_z == bl // BLOCK_Z
+    for q in range(3):
+        part = spread[q * ng * 8 : (q + 1) * ng * 8]
+        vector = jnp.sum(jnp.where(mine, part, 0.0), axis=0, keepdims=True)
+        matrix = inverse[...] if q == 1 else inv_recv[q // 2]
+        correction = jnp.sum(matrix * vector, axis=1, keepdims=True)
+        table = jnp.where(placed, jnp.broadcast_to(correction, (size, dz)), 0.0)
+        for k in range(ng):
+            for c in range(3):
+                start = (k * 3 + c) * cells_z
+                f_all[q, k + 1, c : c + 1, :] = jnp.sum(
+                    table[start : start + cells_z], axis=0, keepdims=True
+                )
+
+    def full(q, at, c):
+        return jnp.broadcast_to(f_all[q, at, c : c + 1, :], (dy, dz))
+
+    own_fine = [full(1, g + 1, c) for c in range(3)]
 
     def fill_plane(i, _):
         for c in range(3):
-            u[0, c, i + 1] = jnp.broadcast_to(fx_own[c : c + 1, :], (dy, dz))
+            u[0, c, i + 1] = own_fine[c]
         return 0
 
     lax.fori_loop(0, dx, fill_plane, 0, unroll=UNROLL)
-    for d in range(2):
-        @pl.when(has[d])
-        def _():
-            f_copy(d).wait_recv()
-        @pl.when(sends[d])
-        def _():
-            f_copy(d).wait_send()
     for c in range(3):
-        u[0, c, 0] = jnp.broadcast_to(fx_recv[0, c : c + 1, :], (dy, dz))
-        u[0, c, dx + 1] = jnp.broadcast_to(fx_recv[1, c : c + 1, :], (dy, dz))
+        u[0, c, 0] = full(0, g + 1, c)
+        u[0, c, dx + 1] = full(2, g + 1, c)
+    it = bcoef(0)
+    exchange_wait(h_copy(CHEB, 1))
     step(
         0,
-        lambda c, i: f_all[g, c : c + 1, :],
-        lambda c, i: f_all[g + 2, c : c + 1, :],
+        lambda c, i: f_all[1, g, c : c + 1, :],
+        lambda c, i: f_all[1, g + 2, c : c + 1, :],
         None,
-        bcoef(0),
+        it,
         CHEB,
+        send=False,
     )
+
+    def fine_on_face(d, near, cross, here, before, after):
+        inv, half, w_low, w_high = [pack_recv[d, k] for k in range(4)]
+        zm, zp = z_near(near)
+        zm = jnp.where(lane == 0, 0.0, 0.5 * (near + zm))
+        zp = jnp.where(lane == dz - 1, 0.0, 0.5 * (near + zp))
+        rim = jnp.where((lane == 0) | (lane == dz - 1), near, 0.0)
+        weight = 2.0 * half + cross + w_low + w_high + zm + zp + rim
+        values = [full(*here, c) for c in range(3)]
+        coupled = half * (values[0] + values[1] + values[2])
+        for c in range(3):
+            fm, fp = z_near(values[c])
+            applied = weight * values[c] + coupled - cross * own_fine[c]
+            applied = applied - zm * fm - zp * fp
+            applied = applied - w_low * full(*before, c) - w_high * full(*after, c)
+            recv[CHEB, d, c] = recv[CHEB, d, c] - it * (inv * applied)
+
+    fine_on_face(0, s_recv[0], wx[0], (0, g + 1), (0, g), (0, g + 2))
+    fine_on_face(1, s_recv[1], 0.5 * (s_recv[1] + s_send_up[...]), (2, g + 1), (2, g), (2, g + 2))
+    fine_on_face(2, s_recv[2], 0.5 * (s_recv[2] + s_send_y[1]), (1, g), (0, g), (2, g))
+    fine_on_face(3, s_recv[3], 0.5 * (s_recv[3] + s_send_y[0]), (1, g + 2), (0, g + 2), (2, g + 2))
+    place_halo(CHEB, 1)
+
     slot = 1
     for turn in range(CHEB):
-        halo_wait(CHEB + turn, slot)
+        if turn > 0:
+            halo_wait(CHEB + turn, slot)
         low, high = recv_rows(CHEB + turn)
         if turn + 1 < CHEB:
             step(slot, low, high, bcoef(8 + 2 * turn), bcoef(9 + 2 * turn), CHEB + turn + 1)
@@ -434,9 +536,14 @@
     f32 = jnp.float32
     vmem = pl.BlockSpec(memory_space=pltpu.VMEM)
     smem = pl.BlockSpec(memory_space=pltpu.SMEM)
+    hbm = pl.BlockSpec(memory_space=pltpu.HBM)
     dma = pltpu.SemaphoreType.DMA
     grid = pltpu.VMEM((dx, dy, dz), f32)
+    cg = inverse.shape[1]
     scratch = [
+        pltpu.VMEM((3, dx, dy, dz), f32),
+        pltpu.VMEM((dx, dy, dz), jnp.int32),
+        pltpu.VMEM((cg, cg), f32),
         pltpu.VMEM((2, 3, dx + 2, dy, dz), f32),
         pltpu.VMEM((3, dx, dy, dz), f32),
         pltpu.VMEM((dx + 2, dy, dz), f32),
@@ -456,15 +563,19 @@
         pltpu.VMEM((8, dz), f32),
         pltpu.VMEM((nb, 8, dz), f32),
         pltpu.VMEM((8, dz), f32),
-        pltpu.VMEM((ng, 8, dz), f32),
-        pltpu.VMEM((ng + 2, 8, dz), f32),
-        pltpu.VMEM((8, dz), f32),
-        pltpu.VMEM((2, 8, dz), f32),
+        pltpu.VMEM((3, ng, 8, dz), f32),
+        pltpu.VMEM((3, ng + 2, 8, dz), f32),
+        pltpu.VMEM((2, cg, cg), f32),
+        pltpu.VMEM((4, 4, dx, dz), f32),
+        pltpu.VMEM((4, dy, dz), f32),
+        pltpu.VMEM((4, 4, dx, dz), f32),
+        dma((3,)),
         dma((4,)), dma((4,)),
         dma((ROUNDS, 4)), dma((ROUNDS, 4)),
         dma((ng,)), dma((ng,)),
         dma((nb,)), dma((nb,)),
-        dma((ng,)), dma((ng,)),
+        dma((3 * ng,)), dma((3 * ng,)),
+        dma((4,)), dma((4,)),
         dma((2,)), dma((2,)),
     ]
     return pl.pallas_call(
@@ -473,7 +584,7 @@
             jax.ShapeDtypeStruct(rhs.shape, f32),
             jax.ShapeDtypeStruct(rhs.shape, f32),
         ),
-        in_specs=[vmem, vmem, vmem, smem, smem, smem, vmem],
+        in_specs=[hbm, hbm, vmem, smem, smem, smem, hbm],
         out_specs=(vmem, vmem),
         scratch_shapes=scratch,
         compiler_params=pltpu.CompilerParams(

time: 50.9 us -> 46.7 us (0.917)
  Pallas kernels: 45.2 us -> 40.9 us
    pallas_call x1, Pallas kernels: 45.2 us -> 40.9 us  [per_device(): pl.pallas_call(functools.partial(kernel, nb, ng, dx, dy, dz), out_shape=(...]
where the time goes in v3:
time: 46.7 us; the launch traced here: 46.4 us
  Pallas kernels  40.9 us (88%)
  local copies, waits for them, and re-layouts  4.14 us (9%)
  between operations  1.37 us (3%)
    pallas_call x1, Pallas kernels, per_device(): pl.pallas_call(functools.partial(kernel, nb, ng, dx, dy, dz), out_shape=(...  40.9 us
    unnamed x14, local copies, waits for them, and re-layouts  4.14 us

profile of v3, /device:TPU:0, one launch (start us, length us, event | category | flops | bytes accessed | tf_op | source)
XLA Modules:
  0.0 46.4 jit_solution(10909827649585693828)
XLA Ops:
  0.6 0.0 copy-start.5
  0.6 0.0 copy-start.4
  0.7 0.0 copy-start.3
  1.3 0.0 copy-done.5
  1.3 0.0 copy-done.4
  1.4 0.0 copy-done.3
  1.4 0.0 copy-start
  1.4 1.0 %copy-done = f32[3,16,16,128]{3,2,1,0:T(8,128)S(1)} copy-done((f32[3,16,16,128]{3,2,1,0:T(8,128)S(1)}, f32[3,16,16,128]{3,2,1,0:T(8,128)}, u32[]{:S(2)}) %copy-start) | copy-done | bytes 393240
  2.4 0.0 copy-start.1
  2.4 0.9 %copy-done.1 = s32[16,16,128]{2,1,0:T(8,128)S(1)} copy-done((s32[16,16,128]{2,1,0:T(8,128)S(1)}, s32[16,16,128]{2,1,0:T(8,128)}, u32[]{:S(2)}) %copy-start.1) | copy-done | bytes 131096
  3.3 0.0 copy-start.2
  3.3 0.7 %copy-done.2 = f32[1,48,48]{2,1,0:T(8,128)S(1)} copy-done((f32[1,48,48]{2,1,0:T(8,128)S(1)}, f32[1,48,48]{2,1,0:T(8,128)}, u32[]{:S(2)}) %copy-start.2) | copy-done | bytes 9240
  4.0 40.9 %shard_map.86 = (f32[3,16,16,128]{3,2,1,0:T(8,128)S(1)}, f32[3,16,16,128]{3,2,1,0:T(8,128)S(1)}) custom-call(f32[3,16,16,128]{3,2,1,0:T(8,128)S(1)} %copy-done, s32[16,16,128]{2,1,0:T(8,128)S(1)} %copy-done.1, s32[1,1]{1,0:T(1,128)S(6)} %copy.11.level, s32[1,1,16]{2,1,0:T(1,128)S(1)} %copy-done.3, f32[4]{0:T(128)S(1)} %copy-done.4, f32[4]{0:T(128)S(1)} %copy-done.5, ...), custom_call_target="tpu_custom_call" | custom-call | tf_op jit(solution)/shard_map/pallas_call | solution.py:581
  44.9 0.7 %copy.12 = f32[3,16,16,128]{3,2,1,0:T(8,128)} copy(f32[3,16,16,128]{3,2,1,0:T(8,128)S(1)} %get-tuple-element.4) | data formatting | bytes 786432
  45.7 0.7 %copy.13 = f32[3,16,16,128]{3,2,1,0:T(8,128)} copy(f32[3,16,16,128]{3,2,1,0:T(8,128)S(1)} %get-tuple-element.5) | data formatting | bytes 786432
Async XLA Ops:
  0.6 0.7 %copy-start.5 = (f32[4]{0:T(128)S(1)}, f32[4]{0:T(128)}, u32[]{:S(2)}) copy-start(f32[4]{0:T(128)} %lam.1) | copy-start | bytes 52
  0.6 0.7 %copy-start.4 = (f32[4]{0:T(128)S(1)}, f32[4]{0:T(128)}, u32[]{:S(2)}) copy-start(f32[4]{0:T(128)} %mu.1) | copy-start | bytes 52
  0.7 0.7 %copy-start.3 = (s32[1,1,16]{2,1,0:T(1,128)S(1)}, s32[1,1,16]{2,1,0:T(1,128)}, u32[]{:S(2)}) copy-start(s32[1,1,16]{2,1,0:T(1,128)} %mortar.1) | copy-start | bytes 196
  1.4 1.0 %copy-start = (f32[3,16,16,128]{3,2,1,0:T(8,128)S(1)}, f32[3,16,16,128]{3,2,1,0:T(8,128)}, u32[]{:S(2)}) copy-start(f32[3,16,16,128]{3,2,1,0:T(8,128)} %rhs_in.1) | copy-start | bytes 1179652
  2.4 0.9 %copy-start.1 = (s32[16,16,128]{2,1,0:T(8,128)S(1)}, s32[16,16,128]{2,1,0:T(8,128)}, u32[]{:S(2)}) copy-start(s32[16,16,128]{2,1,0:T(8,128)} %material_in.1) | copy-start | bytes 393220
  3.3 0.7 %copy-start.2 = (f32[1,48,48]{2,1,0:T(8,128)S(1)}, f32[1,48,48]{2,1,0:T(8,128)}, u32[]{:S(2)}) copy-start(f32[1,48,48]{2,1,0:T(8,128)} %inverse_in.1) | copy-start | bytes 27652

commit v4 on v3

--- a/solution.py
+++ b/solution.py
@@ -178,14 +178,27 @@
             )
         return copy
 
+    even = lax.rem(b, 2) == 0
+
     def sweep(plane, turn, slot, carry, unroll):
         carry = plane(0, carry)
         carry = plane(dx - 1, carry)
         if turn is not None:
+            copy = h_copy(turn, slot)
+
+            @pl.when(sends[1] & even)
+            def _():
+                copy(1).start()
+
             for c in range(3):
                 for k in range(dy):
                     up_send[turn, c, k : k + 1, :] = u[slot, c, dx, pl.ds(order[k], 1), :]
-            exchange_start(h_copy(turn, slot), (0, 1))
+            exchange_start(copy, (0,))
+
+            @pl.when(sends[1] & jnp.logical_not(even))
+            def _():
+                copy(1).start()
+
         carry = lax.fori_loop(1, dx - 1, plane, carry, unroll=unroll)
         if turn is not None:
             exchange_start(h_copy(turn, slot), (2, 3))
@@ -578,6 +591,9 @@
         dma((4,)), dma((4,)),
         dma((2,)), dma((2,)),
     ]
+    rhs, material, inverse = (
+        pltpu.with_memory_space_constraint(x, pltpu.HBM) for x in (rhs, material, inverse)
+    )
     return pl.pallas_call(
         functools.partial(kernel, nb, ng, dx, dy, dz),
         out_shape=(

time: 46.7 us -> 43.9 us (0.940)
  local copies, waits for them, and re-layouts: 4.14 us -> 1.51 us
    unnamed x14 -> x8, local copies, waits for them, and re-layouts: 4.14 us -> 1.51 us
where the time goes in v4:
time: 43.9 us; the launch traced here: 43.7 us
  Pallas kernels  40.9 us (93%)
  local copies, waits for them, and re-layouts  1.51 us (3%)
  between operations  1.36 us (3%)
    pallas_call x1, Pallas kernels, per_device(): pl.pallas_call(functools.partial(kernel, nb, ng, dx, dy, dz), out_shape=(...  40.9 us
    unnamed x8, local copies, waits for them, and re-layouts  1.51 us

profile of v4, /device:TPU:0, one launch (start us, length us, event | category | flops | bytes accessed | tf_op | source)
XLA Modules:
  0.0 43.7 jit_solution(6750525834844554438)
XLA Ops:
  0.6 0.0 copy-start.2
  0.6 0.0 copy-start.1
  0.7 0.0 copy-start
  1.3 0.0 copy-done.2
  1.3 0.0 copy-done.1
  1.4 0.0 copy-done
  1.4 40.9 %shard_map.86 = (f32[3,16,16,128]{3,2,1,0:T(8,128)S(1)}, f32[3,16,16,128]{3,2,1,0:T(8,128)S(1)}) custom-call(f32[3,16,16,128]{3,2,1,0:T(8,128)} %rhs_in.1, s32[16,16,128]{2,1,0:T(8,128)} %material_in.1, s32[1,1]{1,0:T(1,128)S(6)} %copy.11.level, s32[1,1,16]{2,1,0:T(1,128)S(1)} %copy-done, f32[4]{0:T(128)S(1)} %copy-done.1, f32[4]{0:T(128)S(1)} %copy-done.2, ...), custom_call_target="tpu_custom_call" | custom-call | tf_op jit(solution)/shard_map/pallas_call | solution.py:597
  42.2 0.7 %copy.12 = f32[3,16,16,128]{3,2,1,0:T(8,128)} copy(f32[3,16,16,128]{3,2,1,0:T(8,128)S(1)} %get-tuple-element.4) | data formatting | bytes 786432
  43.0 0.7 %copy.13 = f32[3,16,16,128]{3,2,1,0:T(8,128)} copy(f32[3,16,16,128]{3,2,1,0:T(8,128)S(1)} %get-tuple-element.5) | data formatting | bytes 786432
Async XLA Ops:
  0.6 0.7 %copy-start.2 = (f32[4]{0:T(128)S(1)}, f32[4]{0:T(128)}, u32[]{:S(2)}) copy-start(f32[4]{0:T(128)} %lam.1) | copy-start | bytes 52
  0.6 0.7 %copy-start.1 = (f32[4]{0:T(128)S(1)}, f32[4]{0:T(128)}, u32[]{:S(2)}) copy-start(f32[4]{0:T(128)} %mu.1) | copy-start | bytes 52
  0.7 0.7 %copy-start = (s32[1,1,16]{2,1,0:T(1,128)S(1)}, s32[1,1,16]{2,1,0:T(1,128)}, u32[]{:S(2)}) copy-start(s32[1,1,16]{2,1,0:T(1,128)} %mortar.1) | copy-start | bytes 196

commit v5 on v4

--- a/solution.py
+++ b/solution.py
@@ -89,8 +89,7 @@
         s_send_y[1, pl.ds(i, 1), :] = plane[0:1]
         return 0
 
-    for k in range(3):
-        fetch(k).wait()
+    fetch(0).wait()
     lax.fori_loop(0, dx, shear_plane, 0, unroll=UNROLL)
     for k in range(dy):
         s_send_up[k : k + 1, :] = shear[dx, pl.ds(order[k], 1), :]
@@ -147,6 +146,8 @@
                 inv_recv[d] = jnp.zeros(inv_recv.shape[1:], jnp.float32)
                 c_all[2 * d] = jnp.zeros(c_all.shape[1:], jnp.float32)
 
+    fetch(1).wait()
+    fetch(2).wait()
     exchange_wait(s_copy)
     shear[0] = s_recv[0]
 
@@ -180,7 +181,10 @@
 
     even = lax.rem(b, 2) == 0
 
-    def sweep(plane, turn, slot, carry, unroll):
+    def sweep(plane, turn, slot, carry, unroll, arrive=None):
+        if arrive is not None:
+            carry = lax.fori_loop(1, dx - 1, plane, carry, unroll=unroll)
+            arrive()
         carry = plane(0, carry)
         carry = plane(dx - 1, carry)
         if turn is not None:
@@ -199,7 +203,8 @@
             def _():
                 copy(1).start()
 
-        carry = lax.fori_loop(1, dx - 1, plane, carry, unroll=unroll)
+        if arrive is None:
+            carry = lax.fori_loop(1, dx - 1, plane, carry, unroll=unroll)
         if turn is not None:
             exchange_start(h_copy(turn, slot), (2, 3))
         return carry
@@ -258,6 +263,12 @@
         exchange_wait(h_copy(turn, slot))
         place_halo(turn, slot)
 
+    def x_arrival(turn, slot):
+        def arrive():
+            exchange_wait(h_copy(turn, slot), (0, 1))
+            place_halo(turn, slot)
+        return arrive
+
     def place_halo(turn, slot):
         for c in range(3):
             u[slot, c, 0] = recv[turn, 0, c]
@@ -371,7 +382,7 @@
         for d in (2, 3):
             recv[1, d, c] = alpha[:dx] * recv[0, d, c] - beta[:dx] * recv[1, d, c]
 
-    def step(slot, low, high, a, c2, following, summed=False, send=True):
+    def step(slot, low, high, a, c2, following, summed=False, send=True, arrive=None):
         other = 1 - slot
 
         def plane(i, sums):
@@ -399,7 +410,7 @@
         init = ()
         if summed:
             init = tuple(jnp.zeros((dy, dz), jnp.float32) for _ in range(3))
-        return sweep(plane, following if send else None, other, init, SWEEP)
+        return sweep(plane, following if send else None, other, init, SWEEP, arrive)
 
     def i_copy(d):
         return remote(inverse, inv_recv.at[d], i_ssem.at[d], i_rsem.at[d], peers[d])
@@ -412,9 +423,14 @@
             slot = 1 - slot
             if turn == 1:
                 exchange_start(i_copy, (0, 1))
-            halo_wait(turn + 1, slot)
+            if turn + 2 < CHEB:
+                halo_wait(turn + 1, slot)
+            else:
+                exchange_wait(h_copy(turn + 1, slot), (2, 3))
         else:
-            sums = step(slot, low, high, None, bcoef(0), CHEB, summed=True)
+            sums = step(
+                slot, low, high, None, bcoef(0), CHEB, summed=True, arrive=x_arrival(turn, slot)
+            )
 
     c_own[...] = jnp.zeros(c_own.shape, jnp.float32)
     for c in range(3):
@@ -532,14 +548,18 @@
 
     slot = 1
     for turn in range(CHEB):
-        if turn > 0:
+        if turn + 1 == CHEB:
+            exchange_wait(h_copy(CHEB + turn, slot), (2, 3))
+        elif turn > 0:
             halo_wait(CHEB + turn, slot)
         low, high = recv_rows(CHEB + turn)
         if turn + 1 < CHEB:
             step(slot, low, high, bcoef(8 + 2 * turn), bcoef(9 + 2 * turn), CHEB + turn + 1)
             slot = 1 - slot
         else:
-            step(slot, low, high, None, None, None)
+            step(
+                slot, low, high, None, None, None, arrive=x_arrival(CHEB + turn, slot)
+            )
 
 
 def per_device(rhs, material, level, mortar, mu, lam, inverse):
@@ -591,8 +611,9 @@
         dma((4,)), dma((4,)),
         dma((2,)), dma((2,)),
     ]
-    rhs, material, inverse = (
-        pltpu.with_memory_space_constraint(x, pltpu.HBM) for x in (rhs, material, inverse)
+    rhs, material, inverse, mortar, mu, lam = (
+        pltpu.with_memory_space_constraint(x, pltpu.HBM)
+        for x in (rhs, material, inverse, mortar, mu, lam)
     )
     return pl.pallas_call(
         functools.partial(kernel, nb, ng, dx, dy, dz),

time: 43.9 us -> 43.3 us (0.986)
  Pallas kernels: 40.9 us -> 40.4 us
    pallas_call x1, Pallas kernels: 40.9 us -> 40.4 us  [per_device(): pl.pallas_call(functools.partial(kernel, nb, ng, dx, dy, dz), out_shape=(...]
    unnamed x8 -> x2, local copies, waits for them, and re-layouts: 1.51 us -> 1.49 us
where the time goes in v5:
time: 43.3 us; the launch traced here: 43.2 us
  Pallas kernels  40.4 us (93%)
  local copies, waits for them, and re-layouts  1.49 us (3%)
  between operations  1.29 us (3%)
    pallas_call x1, Pallas kernels, per_device(): pl.pallas_call(functools.partial(kernel, nb, ng, dx, dy, dz), out_shape=(...  40.4 us
    unnamed x2, local copies, waits for them, and re-layouts  1.49 us

profile of v5, /device:TPU:0, one launch (start us, length us, event | category | flops | bytes accessed | tf_op | source)
XLA Modules:
  0.0 43.2 jit_solution(2242505583547775215)
XLA Ops:
  1.3 40.4 %shard_map.86 = (f32[3,16,16,128]{3,2,1,0:T(8,128)S(1)}, f32[3,16,16,128]{3,2,1,0:T(8,128)S(1)}) custom-call(f32[3,16,16,128]{3,2,1,0:T(8,128)} %rhs_in.1, s32[16,16,128]{2,1,0:T(8,128)} %material_in.1, s32[1,1]{1,0:T(1,128)S(6)} %copy.11.level, s32[1,1,16]{2,1,0:T(1,128)} %mortar.1, f32[4]{0:T(128)} %mu.1, f32[4]{0:T(128)} %lam.1, f32[1,48,48]{2,1,0:T(8,128)} %inverse_in.1), custom_call_target="tpu_custom_call" | custom-call | tf_op jit(solution)/shard_map/pallas_call | solution.py:618
  41.7 0.7 %copy.12 = f32[3,16,16,128]{3,2,1,0:T(8,128)} copy(f32[3,16,16,128]{3,2,1,0:T(8,128)S(1)} %get-tuple-element.4) | data formatting | bytes 786432
  42.4 0.7 %copy.13 = f32[3,16,16,128]{3,2,1,0:T(8,128)} copy(f32[3,16,16,128]{3,2,1,0:T(8,128)S(1)} %get-tuple-element.5) | data formatting | bytes 786432
